TPU v7x, 32 devices: a whole 2x2x4 slice. The times are simulated.
32 devices in a mesh: prompt: 1, seq: 32 (over z, y, x, core).
Axes of the slice: x: 2, y: 2, z: 4, core: 2. Of those that a mesh axis runs over, the one named last changes fastest.
Arguments:
- queries: bfloat16 [8192, 32, 128], P(('prompt', 'seq')), may hold values from -12 to 12
- key_value: bfloat16 [2, 8192, 16, 128], P(None, ('prompt', 'seq')), may hold values from -6 to 6
- damping: bfloat16 [8192], P('prompt'), may hold values from 0.0099487305 to 1
- span_start: int32 [1], P('prompt'), may hold values from 0 to 3584
- steered_heads: int32 [8], replicated, may hold values from 0 to 31, as said below
Outputs:
- attention: bfloat16 [8192, 32, 128], P(('prompt', 'seq'))
Inputs may be any that keep to these rules, and one draw needn't show every extreme that they name: The emphasized tokens are span_start to span_start + 511. `steered_heads`: 8 distinct head numbers in any order; head 31 is always one of them.
All inputs are finite; a program needn't handle non-finite values.
Results may differ from a plain program's by a relative error of at most 0.0085.
Values may be sent and summed in bfloat16 or wider, within the bound.
A program may use at most 64 MiB of HBM per device.

v0:
```python
import jax
import jax.numpy as jnp
from jax import lax
from jax.sharding import PartitionSpec as P

WINDOW = 4096
SPAN = 512


SCORE_SCALE = 144.0 ** (-0.5)
SOFTCAP = 50.0


def piece_terms(query_groups, key_piece, value_piece, key_bias, visible):
    raw_score = jnp.einsum(
        "qkgd,skd->kgqs", query_groups, key_piece, preferred_element_type=jnp.float32
    )
    scores = SOFTCAP * jnp.tanh(raw_score * SCORE_SCALE / SOFTCAP) + key_bias
    weight = jnp.where(visible, jnp.exp(scores), 0.0)
    weight_sum = jnp.sum(weight, axis=-1)
    rounded = weight.astype(jnp.bfloat16)
    weighted = jnp.einsum(
        "kgqs,skd->kgqd", rounded, value_piece, preferred_element_type=jnp.float32
    )
    return (weighted, weight_sum)


def window_part(
    query_groups, window_states, window_log, query_index, key_index, span_first, steer_grid
):
    emphasis = (key_index >= span_first) & (key_index < span_first + SPAN)
    distance = query_index[:, None] - key_index[None, :]
    visible = (key_index[None, :] >= 0) & (distance >= 0) & (distance < WINDOW)
    key_bias = jnp.where(
        steer_grid & ~emphasis[None, None, None, :], window_log[None, None, None, :], 0.0
    )
    return piece_terms(
        query_groups, window_states[0], window_states[1], key_bias, visible[None, None]
    )


def per_device(queries, key_value, damping, span_start, steered_heads):
    query_rows, head_count, head_width = queries.shape
    key_heads = key_value.shape[2]
    group_size = head_count // key_heads
    total_rows = damping.shape[0]
    device_index = lax.axis_index("seq")
    device_count = lax.axis_size("seq")
    span_first = span_start[0]
    log_damping = jnp.log(damping.astype(jnp.float32))
    heads_here = head_count // device_count
    repeated = jnp.repeat(key_value, group_size, axis=2)
    moved_queries, moved_states = (
        lax.all_to_all(
            queries.reshape(1, query_rows, head_count, head_width),
            "seq",
            split_axis=2,
            concat_axis=1,
            tiled=True,
        ),
        lax.all_to_all(repeated, "seq", split_axis=2, concat_axis=1, tiled=True),
    )
    local_heads = device_index * heads_here + jnp.arange(heads_here, dtype=jnp.int32)
    steered = jnp.any(steered_heads[:, None] == local_heads[None, :], axis=0)
    steer_grid = steered[:, None, None, None]
    block_rows = min(512, total_rows)
    padded_states = jnp.pad(moved_states, ((0, 0), (WINDOW, 0), (0, 0), (0, 0)))
    padded_log = jnp.pad(log_damping, (WINDOW, 0))
    span_states = lax.dynamic_slice_in_dim(moved_states, span_first, SPAN, 1)
    span_index = span_first + jnp.arange(SPAN, dtype=jnp.int32)

    def one_block(block_index):
        first_row = block_index * block_rows
        query_index = first_row + jnp.arange(block_rows, dtype=jnp.int32)
        query_groups = lax.dynamic_slice_in_dim(moved_queries[0], first_row, block_rows, 0).reshape(
            block_rows, heads_here, 1, head_width
        )
        window_states = lax.dynamic_slice_in_dim(padded_states, first_row, WINDOW + block_rows, 1)
        window_log = lax.dynamic_slice_in_dim(padded_log, first_row, WINDOW + block_rows, 0)
        key_index = first_row - WINDOW + jnp.arange(WINDOW + block_rows, dtype=jnp.int32)
        weighted, weight_sum = window_part(
            query_groups, window_states, window_log, query_index, key_index, span_first, steer_grid
        )
        span_distance = query_index[:, None] - span_index[None, :]
        span_visible = steer_grid & (span_distance >= WINDOW)[None, None]
        more_weighted, more_sum = piece_terms(
            query_groups, span_states[0], span_states[1], 0.0, span_visible
        )
        result = (weighted + more_weighted) / (weight_sum + more_sum)[..., None]
        result = result.astype(jnp.bfloat16).reshape(heads_here, block_rows, head_width)
        return result.transpose(1, 0, 2)

    blocks = lax.map(one_block, jnp.arange(total_rows // block_rows, dtype=jnp.int32))
    attended = blocks.reshape(total_rows, heads_here, head_width)
    return lax.all_to_all(attended, "seq", split_axis=0, concat_axis=1, tiled=True)


def solution(mesh):
    in_specs = (
        P(("prompt", "seq"), None, None),
        P(None, ("prompt", "seq"), None, None),
        P("prompt"),
        P("prompt"),
        P(),
    )
    out_specs = P(("prompt", "seq"), None, None)
    return jax.shard_map(
        per_device, mesh=mesh, in_specs=in_specs, out_specs=out_specs, check_vma=False
    )
```

profile of v0, /device:TPU:0, one launch (start us, length us, event | category | flops | bytes accessed | tf_op | source)
XLA Modules:
  0.0 517.1 jit_solution(14829330794045654219)
XLA Ops:
  5.1 7.5 %all-to-all-start = ((bf16[2,256,32,128]{3,1,0,2:T(8,128)(2,1)}), bf16[2,256,32,128]{3,1,0,2:T(8,128)(2,1)}, u32[]{:S(2)}, u32[]{:S(2)}) async-start(bf16[2,256,32,128]{3,1,0,2:T(8,128)(2,1)} %bitcast.127), calls=%async_computation | async-start | bytes 8388608 | tf_op jit(solution)/shard_map/all_to_all | solution.py:61
  14.8 91.5 %all-to-all-done = bf16[2,256,32,128]{3,1,0,2:T(8,128)(2,1)} async-done(((bf16[2,256,32,128]{3,1,0,2:T(8,128)(2,1)}), bf16[2,256,32,128]{3,1,0,2:T(8,128)(2,1)}, u32[]{:S(2)}, u32[]{:S(2)}) %all-to-all-start) | async-done | bytes 4194336 | tf_op jit(solution)/shard_map/all_to_all | solution.py:61
  114.3 7.1 %pad_bitcast_fusion = bf16[2,12288,1,128]{3,1,2,0:T(8,128)(2,1)} fusion(bf16[2,8192,1,128]{3,1,0,2:T(8,128)(2,1)S(1)} %bitcast.126), kind=kLoop, calls=%fused_computation.50 | loop fusion | bytes 10485760
  121.4 37.7 %all-to-all-done.1 = bf16[1,256,32,128]{3,1,0,2:T(8,128)(2,1)S(1)} async-done(((bf16[1,256,32,128]{3,1,0,2:T(8,128)(2,1)}), bf16[1,256,32,128]{3,1,0,2:T(8,128)(2,1)S(1)}, u32[]{:S(2)}, u32[]{:S(2)}) %all-to-all-start.1) | async-done | bytes 2097184 | tf_op jit(solution)/shard_map/all_to_all | solution.py:54
  159.1 286.7 %while.15 = (s32[]{:T(128)}, bf16[16,512,1,128]{3,1,2,0:T(8,128)(2,1)}, s32[16]{0:T(128)S(1)}, bf16[2,12288,1,128]{3,1,2,0:T(8,128)(2,1)}, bf16[1,8192,1,128]{3,...) while((s32[]{:T(128)}, ...), condition=%wide.region_4.5_spmd.clone.clone, body=%wide.region_1.4_spmd.clone.clone.sunk | while | flops 1370469888 | bytes 14154046 | solution.py:93
  162.3 8.3 %fusion.65 = (f32[512]{0:T(512)S(1)}, bf16[1,1,512,4608]{2,3,1,0:T(8,128)(2,1)}) fusion(f32[4608]{0:T(1024)S(1)} %dynamic-slice_select_fusion.2, bf16[1,8192,1,128]{3,1,2,0:T(8,128)(2,1)S(1)} %get-tuple-element.388, s32[]{:T(128)S(6)} %select_n.61, bf16[2,12288,1,128]{3,1,2,0:T(8,128)(2,1)} %get-tuple-element.387, s32[]{:T(128)S(6)} %select_n.62, ...), kind=kOutput, calls=%fused_computation.55.clone.1 | convolution fusion | flops 629931520 | bytes 6079496 | tf_op jit(solution)/shard_map/while/body/eval_jaxpr/qkgd,skd->kgqs/dot_general | solution.py:15
  172.3 4.8 fusion.66
  180.3 8.3 %fusion.65 = (f32[512]{0:T(512)S(1)}, bf16[1,1,512,4608]{2,3,1,0:T(8,128)(2,1)}) fusion(f32[4608]{0:T(1024)S(1)} %dynamic-slice_select_fusion.2, bf16[1,8192,1,128]{3,1,2,0:T(8,128)(2,1)S(1)} %get-tuple-element.388, s32[]{:T(128)S(6)} %select_n.61, bf16[2,12288,1,128]{3,1,2,0:T(8,128)(2,1)} %get-tuple-element.387, s32[]{:T(128)S(6)} %select_n.62, ...), kind=kOutput, calls=%fused_computation.55.clone.1 | convolution fusion | flops 629931520 | bytes 6079496 | tf_op jit(solution)/shard_map/while/body/eval_jaxpr/qkgd,skd->kgqs/dot_general | solution.py:15
  190.2 4.8 fusion.66
  198.2 8.3 %fusion.65 = (f32[512]{0:T(512)S(1)}, bf16[1,1,512,4608]{2,3,1,0:T(8,128)(2,1)}) fusion(f32[4608]{0:T(1024)S(1)} %dynamic-slice_select_fusion.2, bf16[1,8192,1,128]{3,1,2,0:T(8,128)(2,1)S(1)} %get-tuple-element.388, s32[]{:T(128)S(6)} %select_n.61, bf16[2,12288,1,128]{3,1,2,0:T(8,128)(2,1)} %get-tuple-element.387, s32[]{:T(128)S(6)} %select_n.62, ...), kind=kOutput, calls=%fused_computation.55.clone.1 | convolution fusion | flops 629931520 | bytes 6079496 | tf_op jit(solution)/shard_map/while/body/eval_jaxpr/qkgd,skd->kgqs/dot_general | solution.py:15
  208.1 4.8 fusion.66
  216.1 8.3 %fusion.65 = (f32[512]{0:T(512)S(1)}, bf16[1,1,512,4608]{2,3,1,0:T(8,128)(2,1)}) fusion(f32[4608]{0:T(1024)S(1)} %dynamic-slice_select_fusion.2, bf16[1,8192,1,128]{3,1,2,0:T(8,128)(2,1)S(1)} %get-tuple-element.388, s32[]{:T(128)S(6)} %select_n.61, bf16[2,12288,1,128]{3,1,2,0:T(8,128)(2,1)} %get-tuple-element.387, s32[]{:T(128)S(6)} %select_n.62, ...), kind=kOutput, calls=%fused_computation.55.clone.1 | convolution fusion | flops 629931520 | bytes 6079496 | tf_op jit(solution)/shard_map/while/body/eval_jaxpr/qkgd,skd->kgqs/dot_general | solution.py:15
  226.0 4.8 fusion.66
  234.0 8.3 %fusion.65 = (f32[512]{0:T(512)S(1)}, bf16[1,1,512,4608]{2,3,1,0:T(8,128)(2,1)}) fusion(f32[4608]{0:T(1024)S(1)} %dynamic-slice_select_fusion.2, bf16[1,8192,1,128]{3,1,2,0:T(8,128)(2,1)S(1)} %get-tuple-element.388, s32[]{:T(128)S(6)} %select_n.61, bf16[2,12288,1,128]{3,1,2,0:T(8,128)(2,1)} %get-tuple-element.387, s32[]{:T(128)S(6)} %select_n.62, ...), kind=kOutput, calls=%fused_computation.55.clone.1 | convolution fusion | flops 629931520 | bytes 6079496 | tf_op jit(solution)/shard_map/while/body/eval_jaxpr/qkgd,skd->kgqs/dot_general | solution.py:15
  243.9 4.8 fusion.66
  251.9 8.3 %fusion.65 = (f32[512]{0:T(512)S(1)}, bf16[1,1,512,4608]{2,3,1,0:T(8,128)(2,1)}) fusion(f32[4608]{0:T(1024)S(1)} %dynamic-slice_select_fusion.2, bf16[1,8192,1,128]{3,1,2,0:T(8,128)(2,1)S(1)} %get-tuple-element.388, s32[]{:T(128)S(6)} %select_n.61, bf16[2,12288,1,128]{3,1,2,0:T(8,128)(2,1)} %get-tuple-element.387, s32[]{:T(128)S(6)} %select_n.62, ...), kind=kOutput, calls=%fused_computation.55.clone.1 | convolution fusion | flops 629931520 | bytes 6079496 | tf_op jit(solution)/shard_map/while/body/eval_jaxpr/qkgd,skd->kgqs/dot_general | solution.py:15
  261.9 4.8 fusion.66
  269.9 8.3 %fusion.65 = (f32[512]{0:T(512)S(1)}, bf16[1,1,512,4608]{2,3,1,0:T(8,128)(2,1)}) fusion(f32[4608]{0:T(1024)S(1)} %dynamic-slice_select_fusion.2, bf16[1,8192,1,128]{3,1,2,0:T(8,128)(2,1)S(1)} %get-tuple-element.388, s32[]{:T(128)S(6)} %select_n.61, bf16[2,12288,1,128]{3,1,2,0:T(8,128)(2,1)} %get-tuple-element.387, s32[]{:T(128)S(6)} %select_n.62, ...), kind=kOutput, calls=%fused_computation.55.clone.1 | convolution fusion | flops 629931520 | bytes 6079496 | tf_op jit(solution)/shard_map/while/body/eval_jaxpr/qkgd,skd->kgqs/dot_general | solution.py:15
  279.8 4.8 fusion.66
  287.8 8.3 %fusion.65 = (f32[512]{0:T(512)S(1)}, bf16[1,1,512,4608]{2,3,1,0:T(8,128)(2,1)}) fusion(f32[4608]{0:T(1024)S(1)} %dynamic-slice_select_fusion.2, bf16[1,8192,1,128]{3,1,2,0:T(8,128)(2,1)S(1)} %get-tuple-element.388, s32[]{:T(128)S(6)} %select_n.61, bf16[2,12288,1,128]{3,1,2,0:T(8,128)(2,1)} %get-tuple-element.387, s32[]{:T(128)S(6)} %select_n.62, ...), kind=kOutput, calls=%fused_computation.55.clone.1 | convolution fusion | flops 629931520 | bytes 6079496 | tf_op jit(solution)/shard_map/while/body/eval_jaxpr/qkgd,skd->kgqs/dot_general | solution.py:15
  297.7 4.8 fusion.66
  305.7 8.3 %fusion.65 = (f32[512]{0:T(512)S(1)}, bf16[1,1,512,4608]{2,3,1,0:T(8,128)(2,1)}) fusion(f32[4608]{0:T(1024)S(1)} %dynamic-slice_select_fusion.2, bf16[1,8192,1,128]{3,1,2,0:T(8,128)(2,1)S(1)} %get-tuple-element.388, s32[]{:T(128)S(6)} %select_n.61, bf16[2,12288,1,128]{3,1,2,0:T(8,128)(2,1)} %get-tuple-element.387, s32[]{:T(128)S(6)} %select_n.62, ...), kind=kOutput, calls=%fused_computation.55.clone.1 | convolution fusion | flops 629931520 | bytes 6079496 | tf_op jit(solution)/shard_map/while/body/eval_jaxpr/qkgd,skd->kgqs/dot_general | solution.py:15
  315.6 4.8 fusion.66
  323.6 8.3 %fusion.65 = (f32[512]{0:T(512)S(1)}, bf16[1,1,512,4608]{2,3,1,0:T(8,128)(2,1)}) fusion(f32[4608]{0:T(1024)S(1)} %dynamic-slice_select_fusion.2, bf16[1,8192,1,128]{3,1,2,0:T(8,128)(2,1)S(1)} %get-tuple-element.388, s32[]{:T(128)S(6)} %select_n.61, bf16[2,12288,1,128]{3,1,2,0:T(8,128)(2,1)} %get-tuple-element.387, s32[]{:T(128)S(6)} %select_n.62, ...), kind=kOutput, calls=%fused_computation.55.clone.1 | convolution fusion | flops 629931520 | bytes 6079496 | tf_op jit(solution)/shard_map/while/body/eval_jaxpr/qkgd,skd->kgqs/dot_general | solution.py:15
  341.5 8.3 %fusion.65 = (f32[512]{0:T(512)S(1)}, bf16[1,1,512,4608]{2,3,1,0:T(8,128)(2,1)}) fusion(f32[4608]{0:T(1024)S(1)} %dynamic-slice_select_fusion.2, bf16[1,8192,1,128]{3,1,2,0:T(8,128)(2,1)S(1)} %get-tuple-element.388, s32[]{:T(128)S(6)} %select_n.61, bf16[2,12288,1,128]{3,1,2,0:T(8,128)(2,1)} %get-tuple-element.387, s32[]{:T(128)S(6)} %select_n.62, ...), kind=kOutput, calls=%fused_computation.55.clone.1 | convolution fusion | flops 629931520 | bytes 6079496 | tf_op jit(solution)/shard_map/while/body/eval_jaxpr/qkgd,skd->kgqs/dot_general | solution.py:15
  359.5 8.3 %fusion.65 = (f32[512]{0:T(512)S(1)}, bf16[1,1,512,4608]{2,3,1,0:T(8,128)(2,1)}) fusion(f32[4608]{0:T(1024)S(1)} %dynamic-slice_select_fusion.2, bf16[1,8192,1,128]{3,1,2,0:T(8,128)(2,1)S(1)} %get-tuple-element.388, s32[]{:T(128)S(6)} %select_n.61, bf16[2,12288,1,128]{3,1,2,0:T(8,128)(2,1)} %get-tuple-element.387, s32[]{:T(128)S(6)} %select_n.62, ...), kind=kOutput, calls=%fused_computation.55.clone.1 | convolution fusion | flops 629931520 | bytes 6079496 | tf_op jit(solution)/shard_map/while/body/eval_jaxpr/qkgd,skd->kgqs/dot_general | solution.py:15
  377.4 8.3 %fusion.65 = (f32[512]{0:T(512)S(1)}, bf16[1,1,512,4608]{2,3,1,0:T(8,128)(2,1)}) fusion(f32[4608]{0:T(1024)S(1)} %dynamic-slice_select_fusion.2, bf16[1,8192,1,128]{3,1,2,0:T(8,128)(2,1)S(1)} %get-tuple-element.388, s32[]{:T(128)S(6)} %select_n.61, bf16[2,12288,1,128]{3,1,2,0:T(8,128)(2,1)} %get-tuple-element.387, s32[]{:T(128)S(6)} %select_n.62, ...), kind=kOutput, calls=%fused_computation.55.clone.1 | convolution fusion | flops 629931520 | bytes 6079496 | tf_op jit(solution)/shard_map/while/body/eval_jaxpr/qkgd,skd->kgqs/dot_general | solution.py:15
  395.3 8.3 %fusion.65 = (f32[512]{0:T(512)S(1)}, bf16[1,1,512,4608]{2,3,1,0:T(8,128)(2,1)}) fusion(f32[4608]{0:T(1024)S(1)} %dynamic-slice_select_fusion.2, bf16[1,8192,1,128]{3,1,2,0:T(8,128)(2,1)S(1)} %get-tuple-element.388, s32[]{:T(128)S(6)} %select_n.61, bf16[2,12288,1,128]{3,1,2,0:T(8,128)(2,1)} %get-tuple-element.387, s32[]{:T(128)S(6)} %select_n.62, ...), kind=kOutput, calls=%fused_computation.55.clone.1 | convolution fusion | flops 629931520 | bytes 6079496 | tf_op jit(solution)/shard_map/while/body/eval_jaxpr/qkgd,skd->kgqs/dot_general | solution.py:15
  413.2 8.3 %fusion.65 = (f32[512]{0:T(512)S(1)}, bf16[1,1,512,4608]{2,3,1,0:T(8,128)(2,1)}) fusion(f32[4608]{0:T(1024)S(1)} %dynamic-slice_select_fusion.2, bf16[1,8192,1,128]{3,1,2,0:T(8,128)(2,1)S(1)} %get-tuple-element.388, s32[]{:T(128)S(6)} %select_n.61, bf16[2,12288,1,128]{3,1,2,0:T(8,128)(2,1)} %get-tuple-element.387, s32[]{:T(128)S(6)} %select_n.62, ...), kind=kOutput, calls=%fused_computation.55.clone.1 | convolution fusion | flops 629931520 | bytes 6079496 | tf_op jit(solution)/shard_map/while/body/eval_jaxpr/qkgd,skd->kgqs/dot_general | solution.py:15
  431.1 8.3 %fusion.65 = (f32[512]{0:T(512)S(1)}, bf16[1,1,512,4608]{2,3,1,0:T(8,128)(2,1)}) fusion(f32[4608]{0:T(1024)S(1)} %dynamic-slice_select_fusion.2, bf16[1,8192,1,128]{3,1,2,0:T(8,128)(2,1)S(1)} %get-tuple-element.388, s32[]{:T(128)S(6)} %select_n.61, bf16[2,12288,1,128]{3,1,2,0:T(8,128)(2,1)} %get-tuple-element.387, s32[]{:T(128)S(6)} %select_n.62, ...), kind=kOutput, calls=%fused_computation.55.clone.1 | convolution fusion | flops 629931520 | bytes 6079496 | tf_op jit(solution)/shard_map/while/body/eval_jaxpr/qkgd,skd->kgqs/dot_general | solution.py:15
  452.4 52.8 %all_to_all.54 = bf16[32,2,16384]{2,1,0:T(2,128)(2,1)S(1)} all-to-all(bf16[32,2,16384]{2,1,0:T(2,128)(2,1)} %reshape.300), channel_id=1, replica_groups=mesh['prompt'=1,'seq'=32] {'seq'}, dimensions={0} | all-to-all | bytes 4194304 | tf_op jit(solution)/shard_map/all_to_all | solution.py:95
  505.2 6.8 %reshape.301 = bf16[8192,1,128]{2,1,0:T(2,128)(2,1)} reshape(bf16[32,2,16384]{2,1,0:T(2,128)(2,1)S(1)} %all_to_all.54) | data formatting | bytes 4194304
  (157 shorter events, 126.3 us)
Async XLA Ops:
  5.1 7.5 %copy-start = (bf16[256,32,128]{2,1,0:T(8,128)(2,1)S(1)}, bf16[256,32,128]{2,1,0:T(8,128)(2,1)}, u32[]{:S(2)}) copy-start(bf16[256,32,128]{2,1,0:T(8,128)(2,1)} %param.7) | copy-start | bytes 6291460
  5.1 101.2 %all-to-all-start = ((bf16[2,256,32,128]{3,1,0,2:T(8,128)(2,1)}), bf16[2,256,32,128]{3,1,0,2:T(8,128)(2,1)}, u32[]{:S(2)}, u32[]{:S(2)}) async-start(bf16[2,256,32,128]{3,1,0,2:T(8,128)(2,1)} %bitcast.127), calls=%async_computation | async-start | bytes 8388608 | tf_op jit(solution)/shard_map/all_to_all | solution.py:61
  12.6 98.5 %copy-start.1 = (bf16[8192]{0:T(1024)(128)(2,1)S(1)}, bf16[8192]{0:T(1024)(128)(2,1)}, u32[]{:S(2)}) copy-start(bf16[8192]{0:T(1024)(128)(2,1)} %param.9) | copy-start | bytes 49156
  12.6 98.5 %copy-start.2 = (s32[8]{0:T(128)S(1)}, s32[8]{0:T(128)}, u32[]{:S(2)}) copy-start(s32[8]{0:T(128)} %param.11) | copy-start | bytes 100
  106.3 52.9 %all-to-all-start.1 = ((bf16[1,256,32,128]{3,1,0,2:T(8,128)(2,1)}), bf16[1,256,32,128]{3,1,0,2:T(8,128)(2,1)S(1)}, u32[]{:S(2)}, u32[]{:S(2)}) async-start(bf16[1,256,32,128]{3,1,0,2:T(8,128)(2,1)} %bitcast.98), calls=%async_computation.1 | async-start | bytes 4194304 | tf_op jit(solution)/shard_map/all_to_all | solution.py:54
where the time goes:
time: 519 us; the launch traced here: 517 us
  matrix products  235 us (45%)
  waiting for transfers between devices  129 us (25%)
  blocking collectives  52.8 us (10%)
  local copies, waits for them, and re-layouts  40.9 us (8%)
  other arithmetic  36.8 us (7%)
  starting transfers between devices  11.6 us (2%)
  loops' own time  10 us (2%)
    dot_general x32, matrix products, piece_terms(): jnp.einsum('qkgd,skd->kgqs', query_groups, key_piece, preferred_element_t...  153 us
    all_to_all x1, waiting for transfers between devices, per_device(): lax.all_to_all(repeated, 'seq', split_axis=2, concat_axis=1, tiled=True)  91.5 us
    dot_general x32, matrix products, piece_terms(): jnp.einsum('kgqs,skd->kgqd', rounded, value_piece, preferred_element_type...  82.2 us
    all_to_all x1, blocking collectives, per_device(): lax.all_to_all(attended, 'seq', split_axis=0, concat_axis=1, tiled=True)  52.8 us
    all_to_all x1, waiting for transfers between devices, per_device(): lax.all_to_all(queries.reshape(1, query_rows, head_count, head_width), 's...  37.7 us
    unnamed x13, local copies, waits for them, and re-layouts  22.8 us
    select_n x16, other arithmetic, window_part(): jnp.where(steer_grid & ~emphasis[None, None, None, :], window_log[None, N...  21.6 us
  transfers between devices with their start and end apart: 2, of which 2 were waited for; matrix products, arithmetic and copies ran while one was open for 2% of the time, Pallas kernels for 0%

commit v1 on v0

v1 whole, which is shorter than its diff:
```python
import functools

import jax
import jax.numpy as jnp
from jax import lax
from jax.experimental import pallas as pl
from jax.experimental.pallas import tpu as pltpu
from jax.sharding import PartitionSpec as P

WINDOW = 4096
SPAN = 512
SCORE_SCALE = 144.0 ** (-0.5)
SOFTCAP = 50.0
LOG2E = 1.4426950408889634
BLOCK = 512


def raw_scores(q, k):
    return lax.dot_general(q, k, (((1,), (1,)), ((), ())), preferred_element_type=jnp.float32)


def weigh(raw, bias):
    capped = jnp.tanh(raw * (SCORE_SCALE / SOFTCAP)) * (SOFTCAP * LOG2E)
    return jnp.exp2(capped + bias)


def gather_values(weight, v):
    both = jnp.concatenate([v, jnp.ones_like(v)], axis=1)
    return jnp.dot(weight.astype(jnp.bfloat16), both, preferred_element_type=jnp.float32)


def attend(far_blocks, flag_ref, q_ref, k_ref, v_ref, bias_ref, sk_ref, sv_ref, out_ref, acc):
    at = pl.program_id(0)
    q = q_ref[...]
    rows = lax.broadcasted_iota(jnp.int32, (BLOCK, BLOCK), 0)
    columns = lax.broadcasted_iota(jnp.int32, (BLOCK, BLOCK), 1)
    near = columns <= rows

    def keys(block):
        return pl.ds(pl.multiple_of(block * BLOCK, BLOCK), BLOCK)

    def bias_of(block):
        return bias_ref[pl.ds(block, 1), :]

    @pl.when(at < far_blocks)
    def _():
        weight = jnp.where(near, weigh(raw_scores(q, k_ref[keys(at), :]), bias_of(at)), 0.0)
        acc[...] = gather_values(weight, v_ref[keys(at), :])

    @pl.when(at >= far_blocks)
    def _():
        far = at - far_blocks
        raw = jnp.where(
            near, raw_scores(q, k_ref[keys(at), :]), raw_scores(q, k_ref[keys(far), :])
        )
        weight = weigh(raw, jnp.where(near, bias_of(at), bias_of(far)))
        acc[...] = gather_values(
            jnp.where(near, weight, 0.0), v_ref[keys(at), :]
        ) + gather_values(jnp.where(near, 0.0, weight), v_ref[keys(far), :])

    @pl.when((at >= far_blocks) & (flag_ref[0] > 0))
    def _():
        seen = columns + flag_ref[1] + far_blocks * BLOCK <= rows + at * BLOCK
        weight = jnp.where(seen, weigh(raw_scores(q, sk_ref[...]), 0.0), 0.0)
        acc[...] += gather_values(weight, sv_ref[...])

    def whole(block):
        weight = weigh(raw_scores(q, k_ref[keys(block), :]), bias_of(block))
        return gather_values(weight, v_ref[keys(block), :])

    first = jnp.maximum(at - far_blocks + 1, 0)
    count = at - first

    @pl.loop(0, count // 2)
    def _(pair):
        acc[...] += whole(first + 2 * pair) + whole(first + 2 * pair + 1)

    @pl.when(count % 2 == 1)
    def _():
        acc[...] += whole(at - 1)

    total = acc[...]
    out_ref[...] = (total[:, :128] / total[:, 128:]).astype(out_ref.dtype)


def attention_kernel(flags, queries, keys, values, bias, span_keys, span_values):
    total_rows, width = queries.shape
    whole = lambda shape: pl.BlockSpec(
        shape, lambda i, flags: (0,) * len(shape), pipeline_mode=pl.Buffered(1)
    )
    return pl.pallas_call(
        functools.partial(attend, WINDOW // BLOCK),
        out_shape=jax.ShapeDtypeStruct((total_rows, width), jnp.bfloat16),
        grid_spec=pltpu.PrefetchScalarGridSpec(
            num_scalar_prefetch=1,
            grid=(total_rows // BLOCK,),
            in_specs=[
                pl.BlockSpec((BLOCK, width), lambda i, flags: (i, 0)),
                whole(keys.shape),
                whole(values.shape),
                whole(bias.shape),
                whole(span_keys.shape),
                whole(span_values.shape),
            ],
            out_specs=pl.BlockSpec((BLOCK, width), lambda i, flags: (i, 0)),
            scratch_shapes=[pltpu.VMEM((BLOCK, 2 * width), jnp.float32)],
        ),
        compiler_params=pltpu.CompilerParams(dimension_semantics=("arbitrary",)),
        name="attend",
    )(flags, queries, keys, values, bias, span_keys, span_values)


def per_device(queries, key_value, damping, span_start, steered_heads):
    query_rows, head_count, width = queries.shape
    key_heads = key_value.shape[2]
    total_rows = damping.shape[0]
    device = lax.axis_index("seq")
    devices = lax.axis_size("seq")
    pieces = key_value.transpose(2, 0, 1, 3).reshape(2 * key_heads, query_rows, width)
    held = lax.all_to_all(pieces, "seq", split_axis=0, concat_axis=0, tiled=True)
    held = held.reshape(total_rows, width)
    moved_queries = lax.all_to_all(
        queries.transpose(1, 0, 2), "seq", split_axis=0, concat_axis=0, tiled=True
    ).reshape(total_rows, width)
    swap = [(i, i ^ 1) for i in range(devices)]
    other = lax.ppermute(held, "seq", swap)
    odd = device % 2 == 1
    keys = jnp.where(odd, other, held)
    values = jnp.where(odd, held, other)

    span_first = span_start[0]
    steered = jnp.any(steered_heads == device)
    index = jnp.arange(total_rows, dtype=jnp.int32)
    emphasis = (index >= span_first) & (index < span_first + SPAN)
    log_damping = jnp.log(damping.astype(jnp.float32)) * LOG2E
    bias = jnp.where(steered & ~emphasis, log_damping, 0.0).reshape(-1, BLOCK)
    span_keys = lax.dynamic_slice_in_dim(keys, span_first, SPAN, 0)
    span_values = lax.dynamic_slice_in_dim(values, span_first, SPAN, 0)
    flags = jnp.stack([steered.astype(jnp.int32), span_first])
    attended = attention_kernel(
        flags, moved_queries, keys, values, bias, span_keys, span_values
    )
    back = lax.all_to_all(
        attended.reshape(devices, query_rows, width), "seq", split_axis=0, concat_axis=0, tiled=True
    )
    return back.transpose(1, 0, 2)


def solution(mesh):
    in_specs = (
        P(("prompt", "seq"), None, None),
        P(None, ("prompt", "seq"), None, None),
        P("prompt"),
        P("prompt"),
        P(),
    )
    out_specs = P(("prompt", "seq"), None, None)
    return jax.shard_map(
        per_device, mesh=mesh, in_specs=in_specs, out_specs=out_specs, check_vma=False
    )
```

time: 519 us -> 238 us (0.46)
  matrix products: 235 us -> 0 us
  waiting for transfers between devices: 129 us -> 40.2 us
  Pallas kernels: 0 us -> 65.6 us
  blocking collectives: 52.8 us -> 113 us
  other arithmetic: 36.8 us -> 4.45 us
  local copies, waits for them, and re-layouts: 40.9 us -> 9.67 us
  loops' own time: 10 us -> 0 us
  starting transfers between devices: 11.6 us -> 3.9 us
    dot_general x64 -> x0, matrix products: 235 us -> none  [the longest x32 153 us: piece_terms(): jnp.einsum('qkgd,skd->kgqs', query_groups, key_piece, preferred_element_t...]
    all_to_all x2 -> x1, waiting for transfers between devices: 129 us -> 40.2 us  [per_device(): lax.all_to_all(queries.transpose(1, 0, 2), 'seq', split_axis=0, concat_ax...]
    pallas_call x0 -> x1, Pallas kernels: none -> 65.6 us  [attention_kernel(): pl.pallas_call(functools.partial(attend, WINDOW // BLOCK), out_shape=jax....]
    all_to_all x1 -> x2, blocking collectives: 52.8 us -> 113 us  [the longest x1 56.9 us: per_device(): lax.all_to_all(attended.reshape(devices, query_rows, width), 'seq', split...]
    select_n x16 -> x2, other arithmetic: 21.6 us -> 3.14 us  [the longest x1 2.5 us: per_device(): values = jnp.where(odd, held, other)]
    unnamed x13 -> x14, local copies, waits for them, and re-layouts: 22.8 us -> 5.57 us
    add x48 -> x0, other arithmetic: 10.5 us -> none  [the longest x16 10.4 us: per_device(): span_index = span_first + jnp.arange(SPAN, dtype=jnp.int32)]
    another operation x1 -> x0, loops' own time: 10 us -> none  [per_device(): lax.map(one_block, jnp.arange(total_rows // block_rows, dtype=jnp.int32))]
  transfers between devices with their start and end apart: 2 -> 2, of which waited for: 2 -> 1; matrix products, arithmetic and copies ran while one was open for 2% -> 3% of each run, Pallas kernels for 0% -> 0%
where the time goes in v1:
time: 238 us
  blocking collectives  113 us (47%)
  Pallas kernels  65.6 us (28%)
  waiting for transfers between devices  40.2 us (17%)
  local copies, waits for them, and re-layouts  9.67 us (4%)
  other arithmetic  4.45 us (2%)
  starting transfers between devices  3.9 us (2%)
    pallas_call x1, Pallas kernels, attention_kernel(): pl.pallas_call(functools.partial(attend, WINDOW // BLOCK), out_shape=jax....  65.6 us
    all_to_all x1, blocking collectives, per_device(): lax.all_to_all(attended.reshape(devices, query_rows, width), 'seq', split...  56.9 us
    all_to_all x1, blocking collectives, per_device(): lax.all_to_all(pieces, 'seq', split_axis=0, concat_axis=0, tiled=True)  55.8 us
    all_to_all x1, waiting for transfers between devices, per_device(): lax.all_to_all(queries.transpose(1, 0, 2), 'seq', split_axis=0, concat_ax...  40.2 us
    unnamed x14, local copies, waits for them, and re-layouts  5.57 us
  transfers between devices with their start and end apart: 2, of which 1 were waited for; matrix products, arithmetic and copies ran while one was open for 3% of the time, Pallas kernels for 0%

profile of v1, /device:TPU:0, one launch (start us, length us, event | category | flops | bytes accessed | tf_op | source)
XLA Modules:
  0.0 237.9 jit_solution(7074191203221298468)
XLA Ops:
  0.0 2.1 copy.12
  2.1 0.0 copy-start.3
  2.1 55.8 %all_to_all.15 = bf16[32,256,128]{2,1,0:T(8,128)(2,1)S(1)} all-to-all(bf16[32,256,128]{2,1,0:T(8,128)(2,1)S(1)} %bitcast.21), channel_id=1, replica_groups=mesh['prompt'=1,'seq'=32] {'seq'}, dimensions={0} | all-to-all | bytes 4194304 | tf_op jit(solution)/shard_map/all_to_all | solution.py:120
  58.0 0.0 copy-start.2
  58.0 0.0 collective-permute-start
  58.0 0.0 copy-done.3
  58.0 2.1 copy.15
  60.1 0.0 copy-done.2
  60.1 0.0 copy-start.5
  60.1 0.0 copy-start.4
  60.1 3.9 %all-to-all-start = ((bf16[32,256,128]{2,1,0:T(8,128)(2,1)}), bf16[32,256,128]{2,1,0:T(8,128)(2,1)}, u32[]{:S(2)}, u32[]{:S(2)}) async-start(bf16[32,256,128]{2,1,0:T(8,128)(2,1)} %bitcast.13), calls=%async_computation | async-start | bytes 4194304 | tf_op jit(solution)/shard_map/all_to_all | solution.py:122
  64.7 0.0 copy-done.5
  64.7 0.6 compare_reduce_fusion
  66.0 0.0 copy-done.4
  66.0 0.6 multiply_select_fusion
  66.6 0.6 reshape.18.bias_ref
  67.2 0.7 pad_add_fusion.flag_ref
  67.9 0.0 collective-permute-done
  67.9 2.5 %broadcast_select_fusion = (bf16[8192,128]{1,0:T(8,128)(2,1)S(1)}, bf16[8192,128]{1,0:T(8,128)(2,1)S(1)}) fusion(bf16[8192,128]{1,0:T(8,128)(2,1)} %collective-permute-done, pred[]{:T(512)S(6)} %eq.13, bf16[32,256,128]{2,1,0:T(8,128)(2,1)} %copy-done.2), kind=kLoop, calls=%fused_computation.1 | loop fusion | flops 2097152 | bytes 8388609 | tf_op jit(solution)/shard_map/jit(_where)/select_n | solution.py:129
  70.4 0.0 copy-start.1
  70.4 0.0 copy-start
  70.4 1.3 copy-done.1
  71.7 0.8 constant_dynamic-slice_fusion
  72.5 40.2 %all-to-all-done = bf16[32,256,128]{2,1,0:T(8,128)(2,1)} async-done(((bf16[32,256,128]{2,1,0:T(8,128)(2,1)}), bf16[32,256,128]{2,1,0:T(8,128)(2,1)}, u32[]{:S(2)}, u32[]{:S(2)}) %all-to-all-start) | async-done | bytes 2097184 | tf_op jit(solution)/shard_map/all_to_all | solution.py:122
  112.7 0.0 copy-done
  112.7 65.6 %attend.1 = bf16[8192,128]{1,0:T(8,128)(2,1)} custom-call(s32[2]{0:T(128)} %pad_add_fusion.flag_ref, bf16[8192,128]{1,0:T(8,128)(2,1)} %bitcast.2.q_ref, bf16[8192,128]{1,0:T(8,128)(2,1)} %copy-done.1, bf16[8192,128]{1,0:T(8,128)(2,1)} %copy-done, f32[16,512]{1,0:T(8,128)} %reshape.18.bias_ref, bf16[512,128]{1,0:T(8,128)(2,1)} %get-tuple-element.8.sk_ref, ...), custom_call_target="tpu_custom_call" | custom-call | tf_op jit(solution)/shard_map/attend/pallas_call | solution.py:91
  178.3 56.9 %all_to_all.16 = bf16[32,256,128]{2,1,0:T(8,128)(2,1)S(1)} all-to-all(bf16[32,256,128]{2,1,0:T(8,128)(2,1)} %bitcast.19), channel_id=1, replica_groups=mesh['prompt'=1,'seq'=32] {'seq'}, dimensions={0} | all-to-all | bytes 4194304 | tf_op jit(solution)/shard_map/all_to_all | solution.py:143
  235.2 2.7 %copy.13 = bf16[256,32,128]{2,1,0:T(8,128)(2,1)} copy(bf16[256,32,128]{2,0,1:T(8,128)(2,1)S(1)} %bitcast.20) | data formatting | bytes 4194304 | tf_op jit(solution)/shard_map/transpose | solution.py:146
Async XLA Ops:
  2.1 55.8 %copy-start.3 = (bf16[256,32,128]{2,1,0:T(8,128)(2,1)S(1)}, bf16[256,32,128]{2,1,0:T(8,128)(2,1)}, u32[]{:S(2)}) copy-start(bf16[256,32,128]{2,1,0:T(8,128)(2,1)} %param.5) | copy-start | bytes 6291460
  58.0 2.1 copy-start.2
  58.0 10.0 %collective-permute-start = (bf16[8192,128]{1,0:T(8,128)(2,1)S(1)}, bf16[8192,128]{1,0:T(8,128)(2,1)}, u32[]{:S(2)}, u32[]{:S(2)}) collective-permute-start(bf16[8192,128]{1,0:T(8,128)(2,1)S(1)} %bitcast.22), channel_id=1, source_target_pairs={{0,1},{1,0},{2,3},{3,2},{4,5},{5,4},{6,7},{7,6},{8,9},{9,8},{10,11... | collective-permute-start | bytes 6291464 | tf_op jit(solution)/shard_map/ppermute | solution.py:126
  60.1 4.6 %copy-start.5 = (s32[8]{0:T(128)S(1)}, s32[8]{0:T(128)}, u32[]{:S(2)}) copy-start(s32[8]{0:T(128)} %param.9) | copy-start | bytes 100
  60.1 5.9 %copy-start.4 = (bf16[8192]{0:T(1024)(128)(2,1)S(1)}, bf16[8192]{0:T(1024)(128)(2,1)}, u32[]{:S(2)}) copy-start(bf16[8192]{0:T(1024)(128)(2,1)} %param.7) | copy-start | bytes 49156
  60.1 52.6 %all-to-all-start = ((bf16[32,256,128]{2,1,0:T(8,128)(2,1)}), bf16[32,256,128]{2,1,0:T(8,128)(2,1)}, u32[]{:S(2)}, u32[]{:S(2)}) async-start(bf16[32,256,128]{2,1,0:T(8,128)(2,1)} %bitcast.13), calls=%async_computation | async-start | bytes 4194304 | tf_op jit(solution)/shard_map/all_to_all | solution.py:122
  70.4 1.3 copy-start.1
  70.4 42.3 %copy-start = (bf16[8192,128]{1,0:T(8,128)(2,1)}, bf16[8192,128]{1,0:T(8,128)(2,1)S(1)}, u32[]{:S(2)}) copy-start(bf16[8192,128]{1,0:T(8,128)(2,1)S(1)} %get-tuple-element.5.v_ref) | copy-start | bytes 6291460

commit v2 on v1

v2 whole, which is shorter than its diff:
```python
import functools

import jax
import jax.numpy as jnp
from jax import lax
from jax.experimental import pallas as pl
from jax.experimental.pallas import tpu as pltpu
from jax.sharding import PartitionSpec as P

WINDOW = 4096
SPAN = 512
SCORE_SCALE = 144.0 ** (-0.5)
SOFTCAP = 50.0
LOG2E = 1.4426950408889634
BLOCK = 512
PIECE = 512
PARTS = 2


def raw_scores(q, k):
    return lax.dot_general(q, k, (((1,), (1,)), ((), ())), preferred_element_type=jnp.float32)


def weigh(raw, bias):
    capped = jnp.tanh(raw * (SCORE_SCALE / SOFTCAP)) * (SOFTCAP * LOG2E)
    return jnp.exp2(capped + bias)


def gather_values(weight, v):
    both = jnp.concatenate([v, jnp.ones_like(v)], axis=1)
    return jnp.dot(weight.astype(jnp.bfloat16), both, preferred_element_type=jnp.float32)


def attend(part, sub_rows, shard_rows, flag_ref, q_ref, k_ref, v_ref, bias_ref, sk_ref, sv_ref, out_ref, acc):
    at = pl.program_id(0)
    q = q_ref[...]
    wide = bias_ref.shape[1]
    far_blocks = WINDOW // wide

    def token(shape):
        row = lax.broadcasted_iota(jnp.int32, shape, 0)
        return row // sub_rows * shard_rows + row % sub_rows + part * sub_rows

    def near_mask():
        shape = (BLOCK, wide)
        return lax.broadcasted_iota(jnp.int32, shape, 1) <= token(shape)

    def keys(block):
        return pl.ds(pl.multiple_of(block * wide, wide), wide)

    def bias_of(block):
        return bias_ref[pl.ds(block, 1), :]

    @pl.when(at < far_blocks)
    def _():
        weight = weigh(raw_scores(q, k_ref[keys(at), :]), bias_of(at))
        acc[...] = gather_values(jnp.where(near_mask(), weight, 0.0), v_ref[keys(at), :])

    @pl.when(at >= far_blocks)
    def _():
        far = at - far_blocks
        near = near_mask()
        raw = jnp.where(
            near, raw_scores(q, k_ref[keys(at), :]), raw_scores(q, k_ref[keys(far), :])
        )
        weight = weigh(raw, jnp.where(near, bias_of(at), bias_of(far)))
        acc[...] = gather_values(
            jnp.where(near, weight, 0.0), v_ref[keys(at), :]
        ) + gather_values(jnp.where(near, 0.0, weight), v_ref[keys(far), :])

    @pl.when((at >= far_blocks) & (flag_ref[0] > 0))
    def _():
        shape = (BLOCK, SPAN)
        key = lax.broadcasted_iota(jnp.int32, shape, 1) + flag_ref[1] + WINDOW
        weight = weigh(raw_scores(q, sk_ref[...]), 0.0)
        acc[...] += gather_values(
            jnp.where(key <= token(shape) + at * wide, weight, 0.0), sv_ref[...]
        )

    @pl.loop(jnp.maximum(at - far_blocks + 1, 0), at)
    def _(block):
        for piece in range(0, wide, PIECE):
            here = pl.ds(pl.multiple_of(block * wide + piece, PIECE), PIECE)
            weight = weigh(
                raw_scores(q, k_ref[here, :]), bias_ref[pl.ds(block, 1), piece : piece + PIECE]
            )
            acc[...] += gather_values(weight, v_ref[here, :])

    total = acc[...]
    out_ref[...] = (total[:, :128] / total[:, 128:]).astype(out_ref.dtype)


def attention_kernel(part, flags, queries, keys, values, bias, span_keys, span_values, shard_rows):
    part_rows, width = queries.shape
    total_rows = keys.shape[0]
    pairs = part_rows * WINDOW
    whole = lambda shape: pl.BlockSpec(
        shape, lambda i, flags: (0,) * len(shape), pipeline_mode=pl.Buffered(1)
    )
    return pl.pallas_call(
        functools.partial(attend, part, shard_rows // PARTS, shard_rows),
        out_shape=jax.ShapeDtypeStruct((part_rows, width), jnp.bfloat16),
        grid_spec=pltpu.PrefetchScalarGridSpec(
            num_scalar_prefetch=1,
            grid=(part_rows // BLOCK,),
            in_specs=[
                pl.BlockSpec((BLOCK, width), lambda i, flags: (i, 0)),
                whole(keys.shape),
                whole(values.shape),
                whole(bias.shape),
                whole(span_keys.shape),
                whole(span_values.shape),
            ],
            out_specs=pl.BlockSpec((BLOCK, width), lambda i, flags: (i, 0)),
            scratch_shapes=[pltpu.VMEM((BLOCK, 2 * width), jnp.float32)],
        ),
        compiler_params=pltpu.CompilerParams(dimension_semantics=("arbitrary",)),
        cost_estimate=pl.CostEstimate(
            flops=6 * pairs * width,
            transcendentals=2 * pairs,
            bytes_accessed=4 * (part_rows + total_rows) * width,
        ),
        name=f"attend_{part}",
    )(flags, queries, keys, values, bias, span_keys, span_values)


def per_device(queries, key_value, damping, span_start, steered_heads):
    query_rows, head_count, width = queries.shape
    key_heads = key_value.shape[2]
    total_rows = damping.shape[0]
    device = lax.axis_index("seq")
    devices = lax.axis_size("seq")
    pieces = key_value.transpose(2, 0, 1, 3).reshape(2 * key_heads, query_rows, width)
    held = lax.all_to_all(pieces, "seq", split_axis=0, concat_axis=0, tiled=True)
    held = held.reshape(total_rows, width)
    sub_rows = query_rows // PARTS
    query_pieces = [
        queries[part * sub_rows : (part + 1) * sub_rows].transpose(1, 0, 2)
        for part in range(PARTS)
    ]

    def exchange(pieces):
        return lax.all_to_all(pieces, "seq", split_axis=0, concat_axis=0, tiled=True)

    moved = [exchange(query_pieces[0])]
    swap = [(i, i ^ 1) for i in range(devices)]
    other = lax.ppermute(held, "seq", swap)
    odd = device % 2 == 1
    keys = jnp.where(odd, other, held)
    values = jnp.where(odd, held, other)

    span_first = span_start[0]
    steered = jnp.any(steered_heads == device)
    index = jnp.arange(total_rows, dtype=jnp.int32)
    emphasis = (index >= span_first) & (index < span_first + SPAN)
    log_damping = jnp.log(damping.astype(jnp.float32)) * LOG2E
    bias = jnp.where(steered & ~emphasis, log_damping, 0.0).reshape(-1, BLOCK * PARTS)
    span_keys = lax.dynamic_slice_in_dim(keys, span_first, SPAN, 0)
    span_values = lax.dynamic_slice_in_dim(values, span_first, SPAN, 0)
    flags = jnp.stack([steered.astype(jnp.int32), span_first])
    back = []
    for part in range(PARTS):
        if part + 1 < PARTS:
            later, moved[part] = lax.optimization_barrier((query_pieces[part + 1], moved[part]))
            moved.append(exchange(later))
        attended = attention_kernel(
            part,
            flags,
            moved[part].reshape(devices * sub_rows, width),
            keys,
            values,
            bias,
            span_keys,
            span_values,
            query_rows,
        )
        back.append(exchange(attended.reshape(devices, sub_rows, width)))
    return jnp.concatenate(back, axis=1).transpose(1, 0, 2)


def solution(mesh):
    in_specs = (
        P(("prompt", "seq"), None, None),
        P(None, ("prompt", "seq"), None, None),
        P("prompt"),
        P("prompt"),
        P(),
    )
    out_specs = P(("prompt", "seq"), None, None)
    return jax.shard_map(
        per_device, mesh=mesh, in_specs=in_specs, out_specs=out_specs, check_vma=False
    )
```

time: 238 us -> 206 us (0.87)
  blocking collectives: 113 us -> 89.9 us
  waiting for transfers between devices: 40.2 us -> 20.9 us
  starting transfers between devices: 3.9 us -> 15.4 us
    all_to_all x1, blocking collectives: 56.9 us -> 34.1 us  [exchange(): lax.all_to_all(pieces, 'seq', split_axis=0, concat_axis=0, tiled=True)]
    all_to_all x1 -> x3, waiting for transfers between devices: 40.2 us -> 20.9 us  [exchange(): lax.all_to_all(pieces, 'seq', split_axis=0, concat_axis=0, tiled=True)]
    all_to_all x1 -> x3, starting transfers between devices: 3.9 us -> 15.4 us  [exchange(): lax.all_to_all(pieces, 'seq', split_axis=0, concat_axis=0, tiled=True)]
    pallas_call x1 -> x2, Pallas kernels: 65.6 us -> 63.5 us  [attention_kernel(): pl.pallas_call(functools.partial(attend, part, shard_rows // PARTS, shard...]
    unnamed x14 -> x15, local copies, waits for them, and re-layouts: 5.57 us -> 6.21 us
  transfers between devices with their start and end apart: 2 -> 4, of which waited for: 1 -> 1; matrix products, arithmetic and copies ran while one was open for 3% -> 4% of each run, Pallas kernels for 0% -> 31%
where the time goes in v2:
time: 206 us
  blocking collectives  89.9 us (44%)
  Pallas kernels  63.5 us (31%)
  waiting for transfers between devices  20.9 us (10%)
  starting transfers between devices  15.4 us (7%)
  local copies, waits for them, and re-layouts  10.7 us (5%)
  other arithmetic  4.04 us (2%)
    pallas_call x2, Pallas kernels, attention_kernel(): pl.pallas_call(functools.partial(attend, part, shard_rows // PARTS, shard...  63.5 us
    all_to_all x1, blocking collectives, per_device(): lax.all_to_all(pieces, 'seq', split_axis=0, concat_axis=0, tiled=True)  55.8 us
    all_to_all x1, blocking collectives, exchange(): lax.all_to_all(pieces, 'seq', split_axis=0, concat_axis=0, tiled=True)  34.1 us
    all_to_all x3, waiting for transfers between devices, exchange(): lax.all_to_all(pieces, 'seq', split_axis=0, concat_axis=0, tiled=True)  20.9 us
    all_to_all x3, starting transfers between devices, exchange(): lax.all_to_all(pieces, 'seq', split_axis=0, concat_axis=0, tiled=True)  15.4 us
    unnamed x15, local copies, waits for them, and re-layouts  6.21 us
  transfers between devices with their start and end apart: 4, of which 1 were waited for; matrix products, arithmetic and copies ran while one was open for 4% of the time, Pallas kernels for 31%

profile of v2, /device:TPU:0, one launch (start us, length us, event | category | flops | bytes accessed | tf_op | source)
XLA Modules:
  0.0 205.9 jit_solution(13153581267414279649)
XLA Ops:
  0.0 2.1 %copy.17 = bf16[2,256,16,128]{3,1,0,2:T(8,128)(2,1)S(1)} copy(bf16[2,256,16,128]{3,2,1,0:T(8,128)(2,1)} %param.6) | data formatting | bytes 4194304 | tf_op args[1]
  2.1 0.0 copy-start.2
  2.1 55.8 %all_to_all.25 = bf16[32,256,128]{2,1,0:T(8,128)(2,1)S(1)} all-to-all(bf16[32,256,128]{2,1,0:T(8,128)(2,1)S(1)} %bitcast.25), channel_id=1, replica_groups=mesh['prompt'=1,'seq'=32] {'seq'}, dimensions={0} | all-to-all | bytes 4194304 | tf_op jit(solution)/shard_map/all_to_all | solution.py:134
  58.0 0.0 collective-permute-start
  58.0 0.0 copy-done.2
  58.0 0.4 fusion.3
  58.3 0.0 copy-start.5
  58.3 0.0 copy-start.4
  58.3 1.4 copy.23
  59.7 3.9 %all-to-all-start = ((bf16[32,128,128]{2,1,0:T(8,128)(2,1)}), bf16[32,128,128]{2,1,0:T(8,128)(2,1)}, u32[]{:S(2)}, u32[]{:S(2)}) async-start(bf16[32,128,128]{2,1,0:T(8,128)(2,1)} %bitcast.18), calls=%async_computation | async-start | bytes 2097152 | tf_op jit(solution)/shard_map/all_to_all | solution.py:143
  64.3 0.0 copy-done.5
  64.3 0.7 compare_reduce_fusion
  65.6 0.0 copy-done.4
  65.6 0.6 multiply_select_fusion
  66.2 0.6 reshape.24.bias_ref
  66.9 1.4 copy.24
  68.2 0.7 pad_add_fusion.flag_ref
  68.9 20.9 %all-to-all-done = bf16[32,128,128]{2,1,0:T(8,128)(2,1)} async-done(((bf16[32,128,128]{2,1,0:T(8,128)(2,1)}), bf16[32,128,128]{2,1,0:T(8,128)(2,1)}, u32[]{:S(2)}, u32[]{:S(2)}) %all-to-all-start) | async-done | bytes 1048608 | tf_op jit(solution)/shard_map/all_to_all | solution.py:143
  89.8 3.6 %all-to-all-start.3 = ((bf16[32,128,128]{2,1,0:T(8,128)(2,1)}), bf16[32,128,128]{2,1,0:T(8,128)(2,1)S(1)}, u32[]{:S(2)}, u32[]{:S(2)}) async-start(bf16[32,128,128]{2,1,0:T(8,128)(2,1)} %bitcast.19), calls=%async_computation.3 | async-start | bytes 2097152 | tf_op jit(solution)/shard_map/all_to_all | solution.py:143
  93.4 0.0 collective-permute-done
  93.5 1.9 broadcast_select_fusion
  95.3 0.0 copy-start.1
  95.4 1.3 copy-done
  96.7 0.8 constant_dynamic-slice_fusion
  97.5 31.5 %attend_0.1 = bf16[4096,128]{1,0:T(8,128)(2,1)} custom-call(s32[2]{0:T(128)} %pad_add_fusion.flag_ref, bf16[4096,128]{1,0:T(8,128)(2,1)} %bitcast.3.q_ref, bf16[8192,128]{1,0:T(8,128)(2,1)} %copy-done.1, bf16[8192,128]{1,0:T(8,128)(2,1)} %copy-done, f32[8,1024]{1,0:T(8,128)} %reshape.24.bias_ref, bf16[512,128]{1,0:T(8,128)(2,1)} %get-tuple-element.14.sk_ref, ...), custom_call_target="tpu_custom_call" | custom-call | flops 12884901888 | bytes 6291456 | tf_op jit(solution)/shard_map/attend_0/pallas_call | solution.py:100
  129.0 0.0 all-to-all-done.3
  129.0 7.9 %all-to-all-start.2 = ((bf16[32,128,128]{2,1,0:T(8,128)(2,1)}), bf16[32,128,128]{2,1,0:T(8,128)(2,1)S(1)}, u32[]{:S(2)}, u32[]{:S(2)}) async-start(bf16[32,128,128]{2,1,0:T(8,128)(2,1)} %bitcast.28), calls=%async_computation.2 | async-start | bytes 2097152 | tf_op jit(solution)/shard_map/all_to_all | solution.py:143
  136.9 32.0 %attend_1.1 = bf16[4096,128]{1,0:T(8,128)(2,1)} custom-call(s32[2]{0:T(128)} %pad_add_fusion.flag_ref, bf16[4096,128]{1,0:T(8,128)(2,1)} %bitcast.27, bf16[8192,128]{1,0:T(8,128)(2,1)} %copy-done.1, bf16[8192,128]{1,0:T(8,128)(2,1)} %copy-done, f32[8,1024]{1,0:T(8,128)} %reshape.24.bias_ref, bf16[512,128]{1,0:T(8,128)(2,1)} %get-tuple-element.14.sk_ref, ...), custom_call_target="tpu_custom_call" | custom-call | flops 12884901888 | bytes 6291456 | tf_op jit(solution)/shard_map/attend_1/pallas_call | solution.py:100
  168.9 0.0 all-to-all-done.2
  168.9 34.1 %all_to_all.26 = bf16[32,128,128]{2,1,0:T(8,128)(2,1)S(1)} all-to-all(bf16[32,128,128]{2,1,0:T(8,128)(2,1)} %bitcast.29), channel_id=1, replica_groups=mesh['prompt'=1,'seq'=32] {'seq'}, dimensions={0} | all-to-all | bytes 2097152 | tf_op jit(solution)/shard_map/all_to_all | solution.py:143
  203.0 0.2 maximum_bitcast_fusion
  203.2 2.7 %copy.18 = bf16[256,32,128]{2,1,0:T(8,128)(2,1)} copy(bf16[256,32,128]{2,0,1:T(8,128)(2,1)S(1)} %maximum_bitcast_fusion) | data formatting | bytes 4194304 | tf_op jit(solution)/shard_map/transpose | solution.py:178
  (4 shorter events, 0.0 us)
Async XLA Ops:
  2.1 55.8 %copy-start.2 = (bf16[256,32,128]{2,1,0:T(8,128)(2,1)S(1)}, bf16[256,32,128]{2,1,0:T(8,128)(2,1)}, u32[]{:S(2)}) copy-start(bf16[256,32,128]{2,1,0:T(8,128)(2,1)} %param.5) | copy-start | bytes 6291460
  58.0 35.5 %collective-permute-start = (bf16[8192,128]{1,0:T(8,128)(2,1)S(1)}, bf16[8192,128]{1,0:T(8,128)(2,1)}, u32[]{:S(2)}, u32[]{:S(2)}) collective-permute-start(bf16[8192,128]{1,0:T(8,128)(2,1)S(1)} %bitcast.26), channel_id=1, source_target_pairs={{0,1},{1,0},{2,3},{3,2},{4,5},{5,4},{6,7},{7,6},{8,9},{9,8},{10,11... | collective-permute-start | bytes 6291464 | tf_op jit(solution)/shard_map/ppermute | solution.py:147
  58.3 6.0 %copy-start.5 = (s32[8]{0:T(128)S(1)}, s32[8]{0:T(128)}, u32[]{:S(2)}) copy-start(s32[8]{0:T(128)} %param.9) | copy-start | bytes 100
  58.3 7.3 %copy-start.4 = (bf16[8192]{0:T(1024)(128)(2,1)S(1)}, bf16[8192]{0:T(1024)(128)(2,1)}, u32[]{:S(2)}) copy-start(bf16[8192]{0:T(1024)(128)(2,1)} %param.7) | copy-start | bytes 49156
  59.7 30.1 %all-to-all-start = ((bf16[32,128,128]{2,1,0:T(8,128)(2,1)}), bf16[32,128,128]{2,1,0:T(8,128)(2,1)}, u32[]{:S(2)}, u32[]{:S(2)}) async-start(bf16[32,128,128]{2,1,0:T(8,128)(2,1)} %bitcast.18), calls=%async_computation | async-start | bytes 2097152 | tf_op jit(solution)/shard_map/all_to_all | solution.py:143
  89.8 39.2 %all-to-all-start.3 = ((bf16[32,128,128]{2,1,0:T(8,128)(2,1)}), bf16[32,128,128]{2,1,0:T(8,128)(2,1)S(1)}, u32[]{:S(2)}, u32[]{:S(2)}) async-start(bf16[32,128,128]{2,1,0:T(8,128)(2,1)} %bitcast.19), calls=%async_computation.3 | async-start | bytes 2097152 | tf_op jit(solution)/shard_map/all_to_all | solution.py:143
  95.3 1.3 copy-start
  95.3 2.1 %copy-start.1 = (bf16[8192,128]{1,0:T(8,128)(2,1)}, bf16[8192,128]{1,0:T(8,128)(2,1)S(1)}, u32[]{:S(2)}) copy-start(bf16[8192,128]{1,0:T(8,128)(2,1)S(1)} %get-tuple-element.10.k_ref) | copy-start | bytes 6291460
  129.0 7.9 %copy-start.3 = (bf16[32,128,128]{2,1,0:T(8,128)(2,1)}, bf16[32,128,128]{2,1,0:T(8,128)(2,1)S(1)}, u32[]{:S(2)}) copy-start(bf16[32,128,128]{2,1,0:T(8,128)(2,1)S(1)} %all-to-all-done.3) | copy-start | bytes 3145732
  129.0 39.9 %all-to-all-start.2 = ((bf16[32,128,128]{2,1,0:T(8,128)(2,1)}), bf16[32,128,128]{2,1,0:T(8,128)(2,1)S(1)}, u32[]{:S(2)}, u32[]{:S(2)}) async-start(bf16[32,128,128]{2,1,0:T(8,128)(2,1)} %bitcast.28), calls=%async_computation.2 | async-start | bytes 2097152 | tf_op jit(solution)/shard_map/all_to_all | solution.py:143

commit v3 on v2

v3 whole, which is shorter than its diff:
```python
import functools

import jax
import jax.numpy as jnp
from jax import lax
from jax.experimental import pallas as pl
from jax.experimental.pallas import tpu as pltpu
from jax.sharding import PartitionSpec as P

WINDOW = 4096
SPAN = 512
SCORE_SCALE = 144.0 ** (-0.5)
SOFTCAP = 50.0
LOG2E = 1.4426950408889634
BLOCK = 512
PIECE = 512
PARTS = 2


def raw_scores(q, k):
    return lax.dot_general(q, k, (((1,), (1,)), ((), ())), preferred_element_type=jnp.float32)


def weigh(raw, bias):
    capped = jnp.tanh(raw * (SCORE_SCALE / SOFTCAP)) * (SOFTCAP * LOG2E)
    return jnp.exp2(capped + bias)


def gather_values(weight, v):
    both = jnp.concatenate([v, jnp.ones_like(v)], axis=1)
    return jnp.dot(weight.astype(jnp.bfloat16), both, preferred_element_type=jnp.float32)


def attend(
    part, sub_rows, shard_rows, devices,
    span_ref, q_ref, k_ref, v_ref, bias_ref, sk_ref, sv_ref, out_ref,
    acc, done, send_sem, recv_sem, own_sem,
):
    me = lax.axis_index("seq")
    wide = bias_ref.shape[1]
    blocks = bias_ref.shape[0]
    far_blocks = WINDOW // wide
    shards = BLOCK // sub_rows
    barrier = pltpu.get_barrier_semaphore()

    @pl.loop(1, devices)
    def _(step):
        pl.semaphore_signal(
            barrier,
            inc=1,
            device_id={"seq": lax.rem(me + step, devices)},
            device_id_type=pl.DeviceIdType.MESH,
        )

    pl.semaphore_wait(barrier, devices - 1)

    def copy_to(target):
        return pltpu.make_async_remote_copy(
            src_ref=done.at[target],
            dst_ref=out_ref.at[me],
            send_sem=send_sem.at[target],
            recv_sem=recv_sem.at[me],
            device_id={"seq": target},
            device_id_type=pl.DeviceIdType.MESH,
        )

    def copy_own():
        return pltpu.make_async_copy(done.at[me], out_ref.at[me], own_sem)

    def token(shape):
        row = lax.broadcasted_iota(jnp.int32, shape, 0)
        return row // sub_rows * shard_rows + row % sub_rows + part * sub_rows

    def near_mask():
        shape = (BLOCK, wide)
        return lax.broadcasted_iota(jnp.int32, shape, 1) <= token(shape)

    def keys(block):
        return pl.ds(pl.multiple_of(block * wide, wide), wide)

    def bias_of(block):
        return bias_ref[pl.ds(block, 1), :]

    def block_at(step):
        return lax.rem(me // shards + step, blocks)

    def send(step):
        first = block_at(step) * shards
        for shard in range(shards):
            target = first + shard

            @pl.when(target != me)
            def _():
                copy_to(target).start()

            @pl.when(target == me)
            def _():
                copy_own().start()

    @pl.loop(0, blocks)
    def _(step):
        at = block_at(step)
        q = q_ref[pl.ds(pl.multiple_of(at * BLOCK, BLOCK), BLOCK), :]

        @pl.when(step > 0)
        def _():
            send(step - 1)

        @pl.when(at < far_blocks)
        def _():
            weight = weigh(raw_scores(q, k_ref[keys(at), :]), bias_of(at))
            acc[...] = gather_values(jnp.where(near_mask(), weight, 0.0), v_ref[keys(at), :])

        @pl.when(at >= far_blocks)
        def _():
            far = at - far_blocks
            near = near_mask()
            raw = jnp.where(
                near, raw_scores(q, k_ref[keys(at), :]), raw_scores(q, k_ref[keys(far), :])
            )
            weight = weigh(raw, jnp.where(near, bias_of(at), bias_of(far)))
            acc[...] = gather_values(
                jnp.where(near, weight, 0.0), v_ref[keys(at), :]
            ) + gather_values(jnp.where(near, 0.0, weight), v_ref[keys(far), :])
            shape = (BLOCK, SPAN)
            key = lax.broadcasted_iota(jnp.int32, shape, 1) + span_ref[...] + WINDOW
            weight = weigh(raw_scores(q, sk_ref[...]), 0.0)
            acc[...] += gather_values(
                jnp.where(key <= token(shape) + at * wide, weight, 0.0), sv_ref[...]
            )

        @pl.loop(jnp.maximum(at - far_blocks + 1, 0), at)
        def _(block):
            for piece in range(0, wide, PIECE):
                here = pl.ds(pl.multiple_of(block * wide + piece, PIECE), PIECE)
                weight = weigh(
                    raw_scores(q, k_ref[here, :]), bias_ref[pl.ds(block, 1), piece : piece + PIECE]
                )
                acc[...] += gather_values(weight, v_ref[here, :])

        total = acc[...]
        result = (total[:, :128] / total[:, 128:]).astype(done.dtype)
        done[pl.ds(at * shards, shards)] = result.reshape(shards, sub_rows, 128)

    send(blocks - 1)
    copy_own().wait()

    @pl.loop(1, devices)
    def _(step):
        other = lax.rem(me + step, devices)
        copy_to(other).wait_send()
        pltpu.make_async_remote_copy(
            src_ref=done.at[other],
            dst_ref=out_ref.at[other],
            send_sem=send_sem.at[other],
            recv_sem=recv_sem.at[other],
            device_id={"seq": other},
            device_id_type=pl.DeviceIdType.MESH,
        ).wait_recv()


def attention_kernel(part, span, queries, keys, values, bias, span_keys, span_values, devices):
    part_rows, width = queries.shape
    total_rows = keys.shape[0]
    shard_rows = total_rows // devices
    sub_rows = part_rows // devices
    pairs = part_rows * WINDOW
    return pl.pallas_call(
        functools.partial(attend, part, sub_rows, shard_rows, devices),
        out_shape=jax.ShapeDtypeStruct((devices, sub_rows, width), jnp.bfloat16),
        in_specs=[pl.BlockSpec(memory_space=pltpu.VMEM)] * 7,
        out_specs=pl.BlockSpec(memory_space=pl.ANY),
        scratch_shapes=[
            pltpu.VMEM((BLOCK, 2 * width), jnp.float32),
            pltpu.VMEM((devices, sub_rows, width), jnp.bfloat16),
            pltpu.SemaphoreType.DMA((devices,)),
            pltpu.SemaphoreType.DMA((devices,)),
            pltpu.SemaphoreType.DMA,
        ],
        compiler_params=pltpu.CompilerParams(collective_id=part, has_side_effects=True),
        cost_estimate=pl.CostEstimate(
            flops=6 * pairs * width,
            transcendentals=2 * pairs,
            bytes_accessed=4 * (part_rows + total_rows) * width,
        ),
        name=f"attend_{part}",
    )(span, queries, keys, values, bias, span_keys, span_values)


def per_device(queries, key_value, damping, span_start, steered_heads):
    query_rows, head_count, width = queries.shape
    key_heads = key_value.shape[2]
    total_rows = damping.shape[0]
    device = lax.axis_index("seq")
    devices = lax.axis_size("seq")
    pieces = key_value.transpose(2, 0, 1, 3).reshape(2 * key_heads, query_rows, width)
    held = lax.all_to_all(pieces, "seq", split_axis=0, concat_axis=0, tiled=True)
    held = held.reshape(total_rows, width)
    sub_rows = query_rows // PARTS
    query_pieces = [
        queries[part * sub_rows : (part + 1) * sub_rows].transpose(1, 0, 2)
        for part in range(PARTS)
    ]

    def exchange(pieces):
        return lax.all_to_all(pieces, "seq", split_axis=0, concat_axis=0, tiled=True)

    moved = [exchange(query_pieces[0])]
    swap = [(i, i ^ 1) for i in range(devices)]
    other = lax.ppermute(held, "seq", swap)
    odd = device % 2 == 1
    keys = jnp.where(odd, other, held)
    values = jnp.where(odd, held, other)

    span_first = span_start[0]
    steered = jnp.any(steered_heads == device)
    index = jnp.arange(total_rows, dtype=jnp.int32)
    emphasis = (index >= span_first) & (index < span_first + SPAN)
    log_damping = jnp.log(damping.astype(jnp.float32)) * LOG2E
    bias = jnp.where(steered & ~emphasis, log_damping, 0.0).reshape(-1, BLOCK * PARTS)
    span_keys = lax.dynamic_slice_in_dim(keys, span_first, SPAN, 0)
    span_values = lax.dynamic_slice_in_dim(values, span_first, SPAN, 0)
    span = jnp.where(steered, span_first, 2 * total_rows).reshape(1, 1)
    back = []
    for part in range(PARTS):
        if part + 1 < PARTS:
            later, moved[part] = lax.optimization_barrier((query_pieces[part + 1], moved[part]))
            moved.append(exchange(later))
        attended = attention_kernel(
            part,
            span,
            moved[part].reshape(devices * sub_rows, width),
            keys,
            values,
            bias,
            span_keys,
            span_values,
            devices,
        )
        back.append(attended)
    return jnp.concatenate(back, axis=1).transpose(1, 0, 2)


def solution(mesh):
    in_specs = (
        P(("prompt", "seq"), None, None),
        P(None, ("prompt", "seq"), None, None),
        P("prompt"),
        P("prompt"),
        P(),
    )
    out_specs = P(("prompt", "seq"), None, None)
    return jax.shard_map(
        per_device, mesh=mesh, in_specs=in_specs, out_specs=out_specs, check_vma=False
    )
```

time: 206 us -> 192 us (0.932); the launches traced: 206 us -> 190 us
  blocking collectives: 89.9 us -> 55.8 us
  Pallas kernels: 63.5 us -> 87 us
  starting transfers between devices: 15.4 us -> 7.71 us
    all_to_all x1 -> x0, blocking collectives: 34.1 us -> none  [exchange(): lax.all_to_all(pieces, 'seq', split_axis=0, concat_axis=0, tiled=True)]
    pallas_call x2, Pallas kernels: 63.5 us -> 87 us  [attention_kernel(): pl.pallas_call(functools.partial(attend, part, sub_rows, shard_rows, devi...]
    all_to_all x3 -> x2, starting transfers between devices: 15.4 us -> 7.7 us  [exchange(): lax.all_to_all(pieces, 'seq', split_axis=0, concat_axis=0, tiled=True)]
    unnamed x15 -> x17, local copies, waits for them, and re-layouts: 6.21 us -> 7.18 us
    all_to_all x3 -> x2, waiting for transfers between devices: 20.9 us -> 21.5 us  [exchange(): lax.all_to_all(pieces, 'seq', split_axis=0, concat_axis=0, tiled=True)]
  transfers between devices with their start and end apart: 4 -> 3, of which waited for: 1 -> 1; matrix products, arithmetic and copies ran while one was open for 4% -> 4% of each run, Pallas kernels for 31% -> 23%
where the time goes in v3:
time: 192 us; the launch traced here: 190 us
  Pallas kernels  87 us (45%)
  blocking collectives  55.8 us (29%)
  waiting for transfers between devices  21.5 us (11%)
  local copies, waits for them, and re-layouts  11.7 us (6%)
  starting transfers between devices  7.71 us (4%)
  other arithmetic  4.58 us (2%)
    pallas_call x2, Pallas kernels, attention_kernel(): pl.pallas_call(functools.partial(attend, part, sub_rows, shard_rows, devi...  87 us
    all_to_all x1, blocking collectives, per_device(): lax.all_to_all(pieces, 'seq', split_axis=0, concat_axis=0, tiled=True)  55.8 us
    all_to_all x2, waiting for transfers between devices, exchange(): lax.all_to_all(pieces, 'seq', split_axis=0, concat_axis=0, tiled=True)  21.5 us
    all_to_all x2, starting transfers between devices, exchange(): lax.all_to_all(pieces, 'seq', split_axis=0, concat_axis=0, tiled=True)  7.7 us
    unnamed x17, local copies, waits for them, and re-layouts  7.18 us
  transfers between devices with their start and end apart: 3, of which 1 were waited for; matrix products, arithmetic and copies ran while one was open for 4% of the time, Pallas kernels for 23%

profile of v3, /device:TPU:0, one launch (start us, length us, event | category | flops | bytes accessed | tf_op | source)
XLA Modules:
  0.0 189.8 jit_solution(7202824036903704098)
XLA Ops:
  0.0 2.1 %copy.15 = bf16[2,256,16,128]{3,1,0,2:T(8,128)(2,1)S(1)} copy(bf16[2,256,16,128]{3,2,1,0:T(8,128)(2,1)} %param.6) | data formatting | bytes 4194304 | tf_op args[1]
  2.1 0.0 copy-start.2
  2.1 55.8 %all_to_all.15 = bf16[32,256,128]{2,1,0:T(8,128)(2,1)S(1)} all-to-all(bf16[32,256,128]{2,1,0:T(8,128)(2,1)S(1)} %bitcast.24), channel_id=1, replica_groups=mesh['prompt'=1,'seq'=32] {'seq'}, dimensions={0} | all-to-all | bytes 4194304 | tf_op jit(solution)/shard_map/all_to_all | solution.py:197
  58.0 0.0 collective-permute-start
  58.0 0.0 copy-done.2
  58.0 0.4 fusion.3
  58.3 0.0 copy-start.6
  58.3 0.0 copy-start.5
  58.3 1.4 copy.21
  59.7 3.9 %all-to-all-start = ((bf16[32,128,128]{2,1,0:T(8,128)(2,1)}), bf16[32,128,128]{2,1,0:T(8,128)(2,1)}, u32[]{:S(2)}, u32[]{:S(2)}) async-start(bf16[32,128,128]{2,1,0:T(8,128)(2,1)} %bitcast.16), calls=%async_computation | async-start | bytes 2097152 | tf_op jit(solution)/shard_map/all_to_all | solution.py:206
  64.3 0.0 copy-done.6
  64.3 0.7 compare_reduce_fusion
  65.0 0.0 copy-done.5
  65.0 0.7 multiply_select_fusion
  65.6 0.6 reshape.22.bias_ref
  66.3 1.4 copy.22
  68.3 21.5 %all-to-all-done = bf16[32,128,128]{2,1,0:T(8,128)(2,1)} async-done(((bf16[32,128,128]{2,1,0:T(8,128)(2,1)}), bf16[32,128,128]{2,1,0:T(8,128)(2,1)}, u32[]{:S(2)}, u32[]{:S(2)}) %all-to-all-start) | async-done | bytes 1048608 | tf_op jit(solution)/shard_map/all_to_all | solution.py:206
  89.8 3.8 %all-to-all-start.2 = ((bf16[32,128,128]{2,1,0:T(8,128)(2,1)}), bf16[32,128,128]{2,1,0:T(8,128)(2,1)S(1)}, u32[]{:S(2)}, u32[]{:S(2)}) async-start(bf16[32,128,128]{2,1,0:T(8,128)(2,1)} %bitcast.17), calls=%async_computation.2 | async-start | bytes 2097152 | tf_op jit(solution)/shard_map/all_to_all | solution.py:206
  93.6 0.0 collective-permute-done
  93.6 1.9 broadcast_select_fusion
  95.5 0.0 copy-start
  95.5 0.0 copy-start.1
  95.5 1.3 copy-done
  96.8 0.8 constant_dynamic-slice_fusion
  97.7 0.0 copy-done.1
  97.7 44.1 %attend_0.1 = bf16[32,128,128]{2,1,0:T(8,128)(2,1)} custom-call(s32[1,1]{1,0:T(1,128)} %bitcast.1.span_ref, bf16[4096,128]{1,0:T(8,128)(2,1)} %bitcast.4.q_ref, bf16[8192,128]{1,0:T(8,128)(2,1)} %copy-done.1, bf16[8192,128]{1,0:T(8,128)(2,1)} %copy-done, f32[8,1024]{1,0:T(8,128)} %reshape.22.bias_ref, bf16[512,128]{1,0:T(8,128)(2,1)} %get-tuple-element.14.sk_ref, ...), custom_call_target="tpu_custom_call" | custom-call | flops 12884901888 | bytes 6291456 | tf_op jit(solution)/shard_map/attend_0/pallas_call | solution.py:168
  141.8 0.0 all-to-all-done.2
  141.8 0.0 copy-start.3
  141.8 1.0 copy-done.3
  142.8 42.9 %attend_1.1 = bf16[32,128,128]{2,1,0:T(8,128)(2,1)} custom-call(s32[1,1]{1,0:T(1,128)} %bitcast.1.span_ref, bf16[4096,128]{1,0:T(8,128)(2,1)} %bitcast.26, bf16[8192,128]{1,0:T(8,128)(2,1)} %copy-done.1, bf16[8192,128]{1,0:T(8,128)(2,1)} %copy-done, f32[8,1024]{1,0:T(8,128)} %reshape.22.bias_ref, bf16[512,128]{1,0:T(8,128)(2,1)} %get-tuple-element.14.sk_ref, ...), custom_call_target="tpu_custom_call" | custom-call | flops 12884901888 | bytes 6291456 | tf_op jit(solution)/shard_map/attend_1/pallas_call | solution.py:168
  185.7 1.4 maximum_bitcast_fusion
  187.1 2.7 %copy.16 = bf16[256,32,128]{2,1,0:T(8,128)(2,1)} copy(bf16[256,32,128]{2,0,1:T(8,128)(2,1)S(1)} %maximum_bitcast_fusion) | data formatting | bytes 4194304 | tf_op jit(solution)/shard_map/transpose | solution.py:241
  (2 shorter events, 0.0 us)
Async XLA Ops:
  2.1 55.8 %copy-start.2 = (bf16[256,32,128]{2,1,0:T(8,128)(2,1)S(1)}, bf16[256,32,128]{2,1,0:T(8,128)(2,1)}, u32[]{:S(2)}) copy-start(bf16[256,32,128]{2,1,0:T(8,128)(2,1)} %param.5) | copy-start | bytes 6291460
  58.0 35.7 %collective-permute-start = (bf16[8192,128]{1,0:T(8,128)(2,1)S(1)}, bf16[8192,128]{1,0:T(8,128)(2,1)}, u32[]{:S(2)}, u32[]{:S(2)}) collective-permute-start(bf16[8192,128]{1,0:T(8,128)(2,1)S(1)} %bitcast.25), channel_id=1, source_target_pairs={{0,1},{1,0},{2,3},{3,2},{4,5},{5,4},{6,7},{7,6},{8,9},{9,8},{10,11... | collective-permute-start | bytes 6291464 | tf_op jit(solution)/shard_map/ppermute | solution.py:210
  58.3 6.0 %copy-start.6 = (s32[8]{0:T(128)S(1)}, s32[8]{0:T(128)}, u32[]{:S(2)}) copy-start(s32[8]{0:T(128)} %param.9) | copy-start | bytes 100
  58.3 6.6 %copy-start.5 = (bf16[8192]{0:T(1024)(128)(2,1)S(1)}, bf16[8192]{0:T(1024)(128)(2,1)}, u32[]{:S(2)}) copy-start(bf16[8192]{0:T(1024)(128)(2,1)} %param.7) | copy-start | bytes 49156
  59.7 30.1 %all-to-all-start = ((bf16[32,128,128]{2,1,0:T(8,128)(2,1)}), bf16[32,128,128]{2,1,0:T(8,128)(2,1)}, u32[]{:S(2)}, u32[]{:S(2)}) async-start(bf16[32,128,128]{2,1,0:T(8,128)(2,1)} %bitcast.16), calls=%async_computation | async-start | bytes 2097152 | tf_op jit(solution)/shard_map/all_to_all | solution.py:206
  89.8 52.0 %all-to-all-start.2 = ((bf16[32,128,128]{2,1,0:T(8,128)(2,1)}), bf16[32,128,128]{2,1,0:T(8,128)(2,1)S(1)}, u32[]{:S(2)}, u32[]{:S(2)}) async-start(bf16[32,128,128]{2,1,0:T(8,128)(2,1)} %bitcast.17), calls=%async_computation.2 | async-start | bytes 2097152 | tf_op jit(solution)/shard_map/all_to_all | solution.py:206
  95.5 1.3 copy-start
  95.5 2.2 %copy-start.1 = (bf16[8192,128]{1,0:T(8,128)(2,1)}, bf16[8192,128]{1,0:T(8,128)(2,1)S(1)}, u32[]{:S(2)}) copy-start(bf16[8192,128]{1,0:T(8,128)(2,1)S(1)} %get-tuple-element.10.k_ref) | copy-start | bytes 6291460
  141.8 1.0 copy-start.3
  142.8 42.9 %copy-start.4 = (bf16[32,128,128]{2,1,0:T(8,128)(2,1)S(1)}, bf16[32,128,128]{2,1,0:T(8,128)(2,1)}, u32[]{:S(2)}) copy-start(bf16[32,128,128]{2,1,0:T(8,128)(2,1)} %attend_0.1) | copy-start | bytes 3145732

commit v4 on v3

--- a/solution.py
+++ b/solution.py
@@ -33,39 +33,53 @@
 
 def attend(
     part, sub_rows, shard_rows, devices,
-    span_ref, q_ref, k_ref, v_ref, bias_ref, sk_ref, sv_ref, out_ref,
-    acc, done, send_sem, recv_sem, own_sem,
+    span_ref, q_ref, k_ref, v_ref, bias_ref, sk_ref, sv_ref, *rest,
 ):
+    sends = part == PARTS - 1
+    if sends:
+        *earlier, out_ref, acc, done, send_sem, recv_sem, own_sem = rest
+    else:
+        done, acc = rest
     me = lax.axis_index("seq")
     wide = bias_ref.shape[1]
     blocks = bias_ref.shape[0]
     far_blocks = WINDOW // wide
     shards = BLOCK // sub_rows
-    barrier = pltpu.get_barrier_semaphore()
-
-    @pl.loop(1, devices)
-    def _(step):
-        pl.semaphore_signal(
-            barrier,
-            inc=1,
-            device_id={"seq": lax.rem(me + step, devices)},
-            device_id_type=pl.DeviceIdType.MESH,
-        )
-
-    pl.semaphore_wait(barrier, devices - 1)
-
-    def copy_to(target):
+
+    def copy_of(turn, source, target, sender):
+        rows = pl.ds(turn * sub_rows, sub_rows)
         return pltpu.make_async_remote_copy(
-            src_ref=done.at[target],
-            dst_ref=out_ref.at[me],
-            send_sem=send_sem.at[target],
-            recv_sem=recv_sem.at[me],
+            src_ref=source.at[target],
+            dst_ref=out_ref.at[sender, rows],
+            send_sem=send_sem.at[turn, target],
+            recv_sem=recv_sem.at[turn, sender],
             device_id={"seq": target},
             device_id_type=pl.DeviceIdType.MESH,
         )
 
-    def copy_own():
-        return pltpu.make_async_copy(done.at[me], out_ref.at[me], own_sem)
+    def copy_own(turn, source):
+        rows = pl.ds(turn * sub_rows, sub_rows)
+        return pltpu.make_async_copy(source.at[me], out_ref.at[me, rows], own_sem.at[turn])
+
+    if sends:
+        barrier = pltpu.get_barrier_semaphore()
+
+        @pl.loop(1, devices)
+        def _(step):
+            pl.semaphore_signal(
+                barrier,
+                inc=1,
+                device_id={"seq": lax.rem(me + step, devices)},
+                device_id_type=pl.DeviceIdType.MESH,
+            )
+
+        pl.semaphore_wait(barrier, devices - 1)
+        for turn, source in enumerate(earlier):
+            copy_own(turn, source).start()
+
+            @pl.loop(1, devices)
+            def _(step):
+                copy_of(turn, source, lax.rem(me + step, devices), me).start()
 
     def token(shape):
         row = lax.broadcasted_iota(jnp.int32, shape, 0)
@@ -91,20 +105,22 @@
 
             @pl.when(target != me)
             def _():
-                copy_to(target).start()
+                copy_of(part, done, target, me).start()
 
             @pl.when(target == me)
             def _():
-                copy_own().start()
+                copy_own(part, done).start()
 
     @pl.loop(0, blocks)
     def _(step):
         at = block_at(step)
         q = q_ref[pl.ds(pl.multiple_of(at * BLOCK, BLOCK), BLOCK), :]
 
-        @pl.when(step > 0)
-        def _():
-            send(step - 1)
+        if sends:
+
+            @pl.when(step > 0)
+            def _():
+                send(step - 1)
 
         @pl.when(at < far_blocks)
         def _():
@@ -142,49 +158,49 @@
         result = (total[:, :128] / total[:, 128:]).astype(done.dtype)
         done[pl.ds(at * shards, shards)] = result.reshape(shards, sub_rows, 128)
 
-    send(blocks - 1)
-    copy_own().wait()
-
-    @pl.loop(1, devices)
-    def _(step):
-        other = lax.rem(me + step, devices)
-        copy_to(other).wait_send()
-        pltpu.make_async_remote_copy(
-            src_ref=done.at[other],
-            dst_ref=out_ref.at[other],
-            send_sem=send_sem.at[other],
-            recv_sem=recv_sem.at[other],
-            device_id={"seq": other},
-            device_id_type=pl.DeviceIdType.MESH,
-        ).wait_recv()
-
-
-def attention_kernel(part, span, queries, keys, values, bias, span_keys, span_values, devices):
+    if sends:
+        send(blocks - 1)
+        for turn, source in enumerate([*earlier, done]):
+            copy_own(turn, source).wait()
+
+            @pl.loop(1, devices)
+            def _(step):
+                other = lax.rem(me + step, devices)
+                copy_of(turn, source, other, me).wait_send()
+                copy_of(turn, source, other, other).wait_recv()
+
+
+def attention_kernel(part, devices, earlier, span, queries, keys, values, bias, *span_states):
     part_rows, width = queries.shape
     total_rows = keys.shape[0]
     shard_rows = total_rows // devices
     sub_rows = part_rows // devices
     pairs = part_rows * WINDOW
+    sends = part == PARTS - 1
+    sending = [
+        pltpu.VMEM((devices, sub_rows, width), jnp.bfloat16),
+        pltpu.SemaphoreType.DMA((PARTS, devices)),
+        pltpu.SemaphoreType.DMA((PARTS, devices)),
+        pltpu.SemaphoreType.DMA((PARTS,)),
+    ] if sends else []
     return pl.pallas_call(
         functools.partial(attend, part, sub_rows, shard_rows, devices),
-        out_shape=jax.ShapeDtypeStruct((devices, sub_rows, width), jnp.bfloat16),
-        in_specs=[pl.BlockSpec(memory_space=pltpu.VMEM)] * 7,
-        out_specs=pl.BlockSpec(memory_space=pl.ANY),
-        scratch_shapes=[
-            pltpu.VMEM((BLOCK, 2 * width), jnp.float32),
-            pltpu.VMEM((devices, sub_rows, width), jnp.bfloat16),
-            pltpu.SemaphoreType.DMA((devices,)),
-            pltpu.SemaphoreType.DMA((devices,)),
-            pltpu.SemaphoreType.DMA,
-        ],
-        compiler_params=pltpu.CompilerParams(collective_id=part, has_side_effects=True),
+        out_shape=jax.ShapeDtypeStruct(
+            (devices, shard_rows if sends else sub_rows, width), jnp.bfloat16
+        ),
+        in_specs=[pl.BlockSpec(memory_space=pltpu.VMEM)] * (7 + len(earlier)),
+        out_specs=pl.BlockSpec(memory_space=pl.ANY if sends else pltpu.VMEM),
+        scratch_shapes=[pltpu.VMEM((BLOCK, 2 * width), jnp.float32)] + sending,
+        compiler_params=pltpu.CompilerParams(
+            collective_id=0 if sends else None, has_side_effects=sends
+        ),
         cost_estimate=pl.CostEstimate(
             flops=6 * pairs * width,
             transcendentals=2 * pairs,
             bytes_accessed=4 * (part_rows + total_rows) * width,
         ),
         name=f"attend_{part}",
-    )(span, queries, keys, values, bias, span_keys, span_values)
+    )(span, queries, keys, values, bias, *span_states, *earlier)
 
 
 def per_device(queries, key_value, damping, span_start, steered_heads):
@@ -221,13 +237,15 @@
     span_keys = lax.dynamic_slice_in_dim(keys, span_first, SPAN, 0)
     span_values = lax.dynamic_slice_in_dim(values, span_first, SPAN, 0)
     span = jnp.where(steered, span_first, 2 * total_rows).reshape(1, 1)
-    back = []
+    earlier = []
     for part in range(PARTS):
         if part + 1 < PARTS:
             later, moved[part] = lax.optimization_barrier((query_pieces[part + 1], moved[part]))
             moved.append(exchange(later))
         attended = attention_kernel(
             part,
+            devices,
+            earlier,
             span,
             moved[part].reshape(devices * sub_rows, width),
             keys,
@@ -235,10 +253,9 @@
             bias,
             span_keys,
             span_values,
-            devices,
         )
-        back.append(attended)
-    return jnp.concatenate(back, axis=1).transpose(1, 0, 2)
+        earlier = [*earlier, attended]
+    return attended.transpose(1, 0, 2)
 
 
 def solution(mesh):

time: 192 us -> 190 us (0.990)
  the two profiles are of different devices: /device:TPU:0 before, /device:TPU:15 now
where the time goes in v4:
time: 190 us; the launch traced here: 189 us
  Pallas kernels  87.9 us (46%)
  blocking collectives  51.7 us (27%)
  waiting for transfers between devices  18.4 us (10%)
  starting transfers between devices  13.5 us (7%)
  local copies, waits for them, and re-layouts  13.3 us (7%)
  other arithmetic  3.29 us (2%)
    pallas_call x2, Pallas kernels, attention_kernel(): pl.pallas_call(functools.partial(attend, part, sub_rows, shard_rows, devi...  87.9 us
    all_to_all x1, blocking collectives, per_device(): lax.all_to_all(pieces, 'seq', split_axis=0, concat_axis=0, tiled=True)  51.7 us
    all_to_all x2, waiting for transfers between devices, exchange(): lax.all_to_all(pieces, 'seq', split_axis=0, concat_axis=0, tiled=True)  18.4 us
    all_to_all x2, starting transfers between devices, exchange(): lax.all_to_all(pieces, 'seq', split_axis=0, concat_axis=0, tiled=True)  12.1 us
    unnamed x15, local copies, waits for them, and re-layouts  7.25 us
    transpose x1, local copies, waits for them, and re-layouts, per_device(): return attended.transpose(1, 0, 2)  4.26 us
  transfers between devices with their start and end apart: 3, of which 1 were waited for; matrix products, arithmetic and copies ran while one was open for 4% of the time, Pallas kernels for 17%

profile of v4, /device:TPU:15, one launch (start us, length us, event | category | flops | bytes accessed | tf_op | source)
XLA Modules:
  0.0 189.5 jit_solution(16889476863720987737)
XLA Ops:
  0.0 2.1 %copy.15 = bf16[2,256,16,128]{3,1,0,2:T(8,128)(2,1)S(1)} copy(bf16[2,256,16,128]{3,2,1,0:T(8,128)(2,1)} %param.6) | data formatting | bytes 4194304 | tf_op args[1]
  2.1 0.0 copy-start.2
  2.1 51.7 %all_to_all.15 = bf16[32,256,128]{2,1,0:T(8,128)(2,1)S(1)} all-to-all(bf16[32,256,128]{2,1,0:T(8,128)(2,1)S(1)} %bitcast.23), channel_id=1, replica_groups=mesh['prompt'=1,'seq'=32] {'seq'}, dimensions={0} | all-to-all | bytes 4194304 | tf_op jit(solution)/shard_map/all_to_all | solution.py:213
  53.8 1.4 collective-permute-start
  55.2 0.0 copy-done.2
  55.2 0.4 fusion.3
  55.6 0.0 copy-start.5
  55.6 0.0 copy-start.4
  55.6 1.4 copy.21
  57.0 5.5 %all-to-all-start = ((bf16[32,128,128]{2,1,0:T(8,128)(2,1)}), bf16[32,128,128]{2,1,0:T(8,128)(2,1)}, u32[]{:S(2)}, u32[]{:S(2)}) async-start(bf16[32,128,128]{2,1,0:T(8,128)(2,1)} %bitcast.15), calls=%async_computation | async-start | bytes 2097152 | tf_op jit(solution)/shard_map/all_to_all | solution.py:222
  63.1 0.0 copy-done.5
  63.2 0.7 compare_reduce_fusion
  63.9 0.0 copy-done.4
  63.9 0.7 multiply_select_fusion
  64.6 0.6 reshape.22.bias_ref
  65.2 1.4 copy.22
  67.3 18.4 %all-to-all-done = bf16[32,128,128]{2,1,0:T(8,128)(2,1)} async-done(((bf16[32,128,128]{2,1,0:T(8,128)(2,1)}), bf16[32,128,128]{2,1,0:T(8,128)(2,1)}, u32[]{:S(2)}, u32[]{:S(2)}) %all-to-all-start) | async-done | bytes 1048608 | tf_op jit(solution)/shard_map/all_to_all | solution.py:222
  85.7 6.7 %all-to-all-start.1 = ((bf16[32,128,128]{2,1,0:T(8,128)(2,1)}), bf16[32,128,128]{2,1,0:T(8,128)(2,1)S(1)}, u32[]{:S(2)}, u32[]{:S(2)}) async-start(bf16[32,128,128]{2,1,0:T(8,128)(2,1)} %bitcast.16), calls=%async_computation.1 | async-start | bytes 2097152 | tf_op jit(solution)/shard_map/all_to_all | solution.py:222
  92.4 0.0 collective-permute-done
  92.4 1.9 broadcast_select_fusion
  94.3 0.0 copy-start
  94.3 0.0 copy-start.1
  94.3 1.3 copy-done
  95.6 0.8 constant_dynamic-slice_fusion
  96.4 0.0 copy-done.1
  96.4 32.3 %attend_0.1.rest_0_ = bf16[32,128,128]{2,1,0:T(8,128)(2,1)} custom-call(s32[1,1]{1,0:T(1,128)} %bitcast.1.span_ref, bf16[4096,128]{1,0:T(8,128)(2,1)} %bitcast.8.q_ref, bf16[8192,128]{1,0:T(8,128)(2,1)} %copy-done.1, bf16[8192,128]{1,0:T(8,128)(2,1)} %copy-done, f32[8,1024]{1,0:T(8,128)} %reshape.22.bias_ref, bf16[512,128]{1,0:T(8,128)(2,1)} %get-tuple-element.14.sk_ref, ...), custom_call_target="tpu_custom_call" | custom-call | flops 12884901888 | bytes 6291456 | tf_op jit(solution)/shard_map/attend_0/pallas_call | solution.py:186
  128.7 0.0 all-to-all-done.1
  128.7 0.0 copy-start.3
  128.7 1.0 copy-done.3
  129.7 55.5 %attend_1.1 = bf16[32,256,128]{2,1,0:T(8,128)(2,1)} custom-call(s32[1,1]{1,0:T(1,128)} %bitcast.1.span_ref, bf16[4096,128]{1,0:T(8,128)(2,1)} %bitcast.26, bf16[8192,128]{1,0:T(8,128)(2,1)} %copy-done.1, bf16[8192,128]{1,0:T(8,128)(2,1)} %copy-done, f32[8,1024]{1,0:T(8,128)} %reshape.22.bias_ref, bf16[512,128]{1,0:T(8,128)(2,1)} %get-tuple-element.14.sk_ref, ...), custom_call_target="tpu_custom_call" | custom-call | flops 12884901888 | bytes 6291456 | tf_op jit(solution)/shard_map/attend_1/pallas_call | solution.py:186
  185.2 4.3 %copy.16 = bf16[256,32,128]{2,1,0:T(8,128)(2,1)} copy(bf16[256,32,128]{2,0,1:T(8,128)(2,1)} %bitcast.25) | data formatting | bytes 4194304 | tf_op jit(solution)/shard_map/transpose | solution.py:258
Async XLA Ops:
  2.1 53.1 %copy-start.2 = (bf16[256,32,128]{2,1,0:T(8,128)(2,1)S(1)}, bf16[256,32,128]{2,1,0:T(8,128)(2,1)}, u32[]{:S(2)}) copy-start(bf16[256,32,128]{2,1,0:T(8,128)(2,1)} %param.5) | copy-start | bytes 6291460
  53.8 38.5 %collective-permute-start = (bf16[8192,128]{1,0:T(8,128)(2,1)S(1)}, bf16[8192,128]{1,0:T(8,128)(2,1)}, u32[]{:S(2)}, u32[]{:S(2)}) collective-permute-start(bf16[8192,128]{1,0:T(8,128)(2,1)S(1)} %bitcast.24), channel_id=1, source_target_pairs={{0,1},{1,0},{2,3},{3,2},{4,5},{5,4},{6,7},{7,6},{8,9},{9,8},{10,11... | collective-permute-start | bytes 6291464 | tf_op jit(solution)/shard_map/ppermute | solution.py:226
  55.6 7.5 %copy-start.5 = (s32[8]{0:T(128)S(1)}, s32[8]{0:T(128)}, u32[]{:S(2)}) copy-start(s32[8]{0:T(128)} %param.9) | copy-start | bytes 100
  55.6 8.3 %copy-start.4 = (bf16[8192]{0:T(1024)(128)(2,1)S(1)}, bf16[8192]{0:T(1024)(128)(2,1)}, u32[]{:S(2)}) copy-start(bf16[8192]{0:T(1024)(128)(2,1)} %param.7) | copy-start | bytes 49156
  57.0 28.7 %all-to-all-start = ((bf16[32,128,128]{2,1,0:T(8,128)(2,1)}), bf16[32,128,128]{2,1,0:T(8,128)(2,1)}, u32[]{:S(2)}, u32[]{:S(2)}) async-start(bf16[32,128,128]{2,1,0:T(8,128)(2,1)} %bitcast.15), calls=%async_computation | async-start | bytes 2097152 | tf_op jit(solution)/shard_map/all_to_all | solution.py:222
  85.7 43.0 %all-to-all-start.1 = ((bf16[32,128,128]{2,1,0:T(8,128)(2,1)}), bf16[32,128,128]{2,1,0:T(8,128)(2,1)S(1)}, u32[]{:S(2)}, u32[]{:S(2)}) async-start(bf16[32,128,128]{2,1,0:T(8,128)(2,1)} %bitcast.16), calls=%async_computation.1 | async-start | bytes 2097152 | tf_op jit(solution)/shard_map/all_to_all | solution.py:222
  94.3 1.3 copy-start
  94.3 2.1 %copy-start.1 = (bf16[8192,128]{1,0:T(8,128)(2,1)}, bf16[8192,128]{1,0:T(8,128)(2,1)S(1)}, u32[]{:S(2)}) copy-start(bf16[8192,128]{1,0:T(8,128)(2,1)S(1)} %get-tuple-element.10.k_ref) | copy-start | bytes 6291460
  128.7 1.0 copy-start.3
